TPU v7x, 32 devices: a whole 2x2x4 slice. The times are simulated.
32 devices in a mesh: freq: 2 (over x), gx: 4 (over y, core), gy: 4 (over z).
Axes of the slice: x: 2, y: 2, z: 4, core: 2. Of those that a mesh axis runs over, the one named last changes fastest.
Arguments:
- wavefield: float32 [8, 2, 512, 512], P('freq', None, 'gx', 'gy'), may hold values from -6 to 6
- velocity: float32 [4, 512, 512], P(None, ('gx', 'freq'), 'gy'), may hold values from 1.5 to 4.5
Outputs:
- image: float32 [4, 512, 512], P(None, 'gx', 'gy')
- extrapolated: float32 [8, 2, 512, 512], P('freq', None, 'gx', 'gy')
All inputs are finite; a program needn't handle non-finite values.
Results may differ from a plain program's by a relative error of at most 0.0001.
Values sent between devices are 32-bit elements; how exact they have to be, the bound alone decides.
No kernel may reach another device: no remote copies, remote signals or barrier semaphores. Data moves between devices by JAX's collectives and lax.ppermute only.
A program may use at most 128 MiB of HBM per device.

v0:
```python
import math

import jax
import jax.numpy as jnp
from jax import lax
from jax.sharding import PartitionSpec as P

ORDER = 8


lowest_freq = 2.0
highest_freq = 60.0
depth_interval = 0.01


def with_halo(cells, sides, width):
    for axis, dim in sides:
        count = lax.axis_size(axis)
        ends = count - 1
        head = lax.slice_in_dim(cells, 0, width, axis=dim)
        tail = lax.slice_in_dim(cells, cells.shape[dim] - width, cells.shape[dim], axis=dim)
        cells = jnp.concatenate(
            [
                lax.ppermute(tail, axis, [(i, (i + 1) % count) for i in range(ends)]),
                cells,
                lax.ppermute(head, axis, [((i + 1) % count, i) for i in range(ends)]),
            ],
            axis=dim,
        )
    return cells


def stencil(source):
    centre = source[..., 1:-1, 1:-1]
    along_x = source[..., 2:, 1:-1] + source[..., :-2, 1:-1]
    along_y = source[..., 1:-1, 2:] + source[..., 1:-1, :-2]
    diagonal_sum = (
        source[..., 2:, 2:] + source[..., 2:, :-2] + source[..., :-2, 2:] + source[..., :-2, :-2]
    )
    return -0.5 * centre + 0.25 * (along_x + along_y) + 0.125 * diagonal_sum


def neighbours(source):
    return stencil(with_halo(source, (("gx", 2), ("gy", 3)), 1))


def term_weights(order):
    values = [1.0 / (term + 1) for term in range(order + 1)]
    whole = sum(values)
    return [value / whole for value in values]


def add_term(real_part, imag_part, part, phase_base, term, weight, order):
    phase = phase_base * ((term + 1) / (order + 1))
    cosine = jnp.cos(phase)
    sine = jnp.sin(phase)
    real_part = real_part + weight * (cosine * part[:, 0] - sine * part[:, 1])
    imag_part = imag_part + weight * (sine * part[:, 0] + cosine * part[:, 1])
    return (real_part, imag_part)


def per_device(wavefield, velocity):
    order = ORDER
    weights = term_weights(order)
    freq_count = wavefield.shape[0]
    freq_total = freq_count * lax.axis_size("freq")
    freq_start = lax.axis_index("freq") * freq_count
    angular = (
        2.0
        * math.pi
        * (
            lowest_freq
            + (highest_freq - lowest_freq)
            * ((freq_start + jnp.arange(freq_count)).astype(jnp.float32) + 0.5)
            / freq_total
        )
    )
    wave_now = wavefield
    image_rows = []
    for depth in range(velocity.shape[0]):
        slowness_tile = lax.all_gather(velocity[depth], "freq", axis=0, tiled=True)
        phase_base = angular[:, None, None] * depth_interval / slowness_tile[None]
        zeros = jnp.zeros(wave_now[:, 0].shape, jnp.float32)
        real_part, imag_part = add_term(zeros, zeros, wave_now, phase_base, 0, weights[0], order)
        previous = wave_now
        present = neighbours(wave_now)
        real_part, imag_part = add_term(
            real_part, imag_part, present, phase_base, 1, weights[1], order
        )
        for term in range(2, order + 1):
            following = 2.0 * neighbours(present) - previous
            previous = present
            present = following
            real_part, imag_part = add_term(
                real_part, imag_part, present, phase_base, term, weights[term], order
            )
        wave_now = jnp.stack([real_part, imag_part], axis=1)
        partial_image = jnp.sum(real_part, axis=0)
        image_rows.append(lax.psum(partial_image, "freq") / math.sqrt(freq_total))
    image = jnp.stack(image_rows)
    return (image, wave_now)


def solution(mesh):
    placed = (P("freq", None, "gx", "gy"), P(None, ("gx", "freq"), "gy"))
    return jax.shard_map(
        per_device,
        mesh=mesh,
        in_specs=placed,
        out_specs=(P(None, "gx", "gy"), P("freq", None, "gx", "gy")),
        check_vma=False,
    )
```

profile of v0, /device:TPU:20, one launch (start us, length us, event | category | flops | bytes accessed | tf_op | source)
XLA Modules:
  0.0 910.4 jit_solution(6786926605230162125)
XLA Ops:
  12.3 2.5 collective-permute-done.1
  19.2 3.5 collective-permute-start.3
  39.9 3.5 collective-permute-start.7
  58.5 3.9 collective-permute-start.11
  71.7 2.5 collective-permute-done.13
  78.9 3.9 collective-permute-start.15
  90.2 2.5 collective-permute-done.17
  98.6 3.9 collective-permute-start.19
  120.1 4.4 collective-permute-start.23
  133.4 2.5 collective-permute-done.25
  141.8 3.9 collective-permute-start.27
  163.7 3.9 collective-permute-start.31
  167.6 4.6 all-gather
  177.4 8.8 fusion.268
  186.3 8.9 fusion.273
  204.9 4.1 collective-permute-start.35
  218.0 2.5 collective-permute-done.37
  223.4 3.9 collective-permute-start.39
  236.5 2.5 collective-permute-done.41
  241.9 3.9 collective-permute-start.43
  262.3 3.9 collective-permute-start.47
  273.5 2.5 collective-permute-done.49
  281.9 3.9 collective-permute-start.51
  303.5 3.9 collective-permute-start.55
  314.3 2.6 collective-permute-start.57
  325.1 3.9 collective-permute-start.59
  346.8 3.9 collective-permute-start.63
  350.8 4.6 all-gather.1
  360.7 8.8 fusion.278
  369.5 8.9 fusion.283
  382.8 2.5 collective-permute-done.65
  391.3 3.9 collective-permute-start.67
  404.5 2.5 collective-permute-done.69
  414.2 4.9 collective-permute-start.71
  439.3 3.9 collective-permute-start.75
  461.1 3.9 collective-permute-start.79
  474.7 2.5 collective-permute-done.81
  483.1 3.9 collective-permute-start.83
  496.8 2.5 collective-permute-done.85
  505.2 3.9 collective-permute-start.87
  527.3 3.9 collective-permute-start.91
  549.6 3.9 collective-permute-start.95
  553.5 4.7 all-gather.2
  564.3 8.8 fusion.288
  573.2 8.9 fusion.331
  586.4 2.5 collective-permute-done.97
  596.0 4.5 collective-permute-start.99
  610.9 2.5 collective-permute-done.101
  620.5 4.5 collective-permute-start.103
  645.3 4.7 collective-permute-start.107
  670.2 4.5 collective-permute-start.111
  695.0 4.5 collective-permute-start.115
  719.7 4.5 collective-permute-start.119
  734.8 4.7 all-gather.3
  746.7 4.5 collective-permute-start.123
  751.2 11.8 %fusion.539 = (f32[128,128]{1,0:T(8,128)}, f32[4,128,128]{2,1,0:T(8,128)}) fusion(f32[4,2,128,128]{3,2,0,1:T(8,128)} %copy-done.95, f32[4,2,128,128]{3,2,0,1:T(8,128)} %copy-done.65, f32[4,2,128,128]{3,2,0,1:T(8,128)} %copy-done.27, f32[4,2,128,128]{3,2,0,1:T(8,128)} %copy-done.25, f32[4,2,128,128]{3,2,0,1:T(8,128)} %copy-done.23, ...), kind=kLoop, calls=%fused_computation.1140 | loop fusion | flops 3522560 | bytes 5111824 | tf_op jit(solution)/shard_map/reduce_sum | solution.py:98
  773.6 2.7 collective-permute-start.125
  776.4 21.5 %fusion.541 = (f32[128,128]{1,0:T(8,128)}, f32[4,128,128]{2,1,0:T(8,128)}, f32[4,128,128]{2,1,0:T(8,128)}) fusion(f32[4,2,128,128]{3,2,0,1:T(8,128)S(1)} %copy-done.92, f32[4,2,128,128]{3,2,0,1:T(8,128)S(1)} %copy-done.39, f32[4,2,128,128]{3,2,0,1:T(8,128)S(1)} %fusion.143, f32[4,2,128,128]{3,2,0,1:T(8,128)S(1)} %fusion.151, ...), kind=kLoop, calls=%fused_computation.1141 | loop fusion | flops 6995968 | bytes 9895952 | tf_op jit(solution)/shard_map/reduce_sum | solution.py:98
  807.7 4.5 collective-permute-start.127
  812.2 24.1 %fusion.526 = (f32[128,128]{1,0:T(8,128)}, f32[4,128,128]{2,1,0:T(8,128)}) fusion(f32[4,128,128]{2,1,0:T(8,128)} %get-tuple-element.15, f32[4,2,128,128]{3,2,0,1:T(8,128)} %copy-done.93, f32[4,2,128,128]{3,2,0,1:T(8,128)} %copy-done.40, f32[4,2,128,128]{3,2,0,1:T(8,128)} %copy-done.15, f32[4,2,128,128]{3,2,0,1:T(8,128)} %copy-done.10, ...), kind=kLoop, calls=%fused_computation.1115 | loop fusion | flops 6995968 | bytes 9633808 | tf_op jit(solution)/shard_map/reduce_sum | solution.py:98
  844.4 9.5 %fusion.263 = f32[4,1,128,128]{3,2,1,0:T(8,128)} fusion(f32[4,1,128,128]{3,2,1,0:T(8,128)S(1)} %copy-done.78, f32[4,1,128,128]{3,2,1,0:T(8,128)S(1)} %fusion.288, f32[4,2,128,128]{3,2,0,1:T(8,128)S(1)} %fusion.3, f32[4,2,128,128]{3,2,0,1:T(8,128)S(1)} %copy-done.74, f32[4,2,128,128]{3,2,0,1:T(8,128)S(1)} %copy-done.61, ...), kind=kLoop, calls=%fused_computation.606 | loop fusion | flops 3473408 | bytes 5046288 | tf_op jit(solution)/shard_map/add | solution.py:58
  854.0 21.3 %fusion.295 = f32[128,128]{1,0:T(8,128)} fusion(f32[4,128,128]{2,1,0:T(8,128)S(1)} %copy-done.102, f32[4,128,128]{2,1,0:T(8,128)S(1)} %copy-done.98, f32[4,2,128,128]{3,2,0,1:T(8,128)S(1)} %fusion.3, f32[4,2,128,128]{3,2,0,1:T(8,128)S(1)} %copy-done.74, f32[4,2,128,128]{3,2,0,1:T(8,128)S(1)} %copy-done.61, f32[4,2,128,128]{3,2,0,1:T(8,128)S(1)} %copy-done.58, ...), kind=kLoop, calls=%fused_computation.640 | loop fusion | flops 9879552 | bytes 9109520 | tf_op jit(solution)/shard_map/reduce_sum | solution.py:98
  876.8 10.6 %fusion.255 = f32[4,1,128,128]{3,2,1,0:T(8,128)S(1)} fusion(f32[4,1,128,128]{3,2,1,0:T(8,128)} %copy-done.75, f32[4,2,128,128]{3,2,0,1:T(8,128)} %copy-done.97, f32[4,2,128,128]{3,2,0,1:T(8,128)} %copy-done.72, f32[4,2,128,128]{3,2,0,1:T(8,128)} %copy-done.59, f32[4,2,128,128]{3,2,0,1:T(8,128)} %copy-done.55, f32[4,2,128,128]{3,2,0,1:T(8,128)} %copy-done.51, ...), kind=kLoop, calls=%fused_computation.598 | loop fusion | flops 3473408 | bytes 5046288 | tf_op jit(solution)/shard_map/add | solution.py:57
  888.3 12.2 %all-reduce.3.cloned.1.call-done = (f32[128,128]{0,1:T(8,128)}, f32[128,128]{0,1:T(8,128)}, f32[128,128]{0,1:T(8,128)}, f32[128,128]{0,1:T(8,128)}) async-done(((f32[128,128]{0,1:T(8,128)}, f32[128,128]{0,1:T(8,128)}, f32[128,128]{0,1:T(8,128)}, f32[128,128]{0,1:T(8,128)}), (f32[128,128]{0,1:T(8,128)}, f32[128,128]{0,1:T(8,128)}, f32[128,128]{0,1:T(8,128)}, ...) | async-done | bytes 262160 | tf_op jit(solution)/shard_map/psum | solution.py:99
  (729 shorter events, 541.0 us)
Async XLA Ops:
  7.2 893.3 %all-reduce.3.cloned.1.call-start = ((), (), s32[]{:S(2)}) async-start(), calls=%async_computation | async-start | bytes 524288 | tf_op jit(solution)/shard_map/psum | solution.py:99
  16.5 6.2 collective-permute-start.2
  19.2 5.5 collective-permute-start.3
  37.2 6.2 collective-permute-start.6
  39.9 5.5 collective-permute-start.7
  56.2 6.2 collective-permute-start.10
  58.5 5.5 collective-permute-start.11
  76.7 6.2 collective-permute-start.14
  78.9 5.5 collective-permute-start.15
  95.3 7.2 collective-permute-start.18
  98.6 5.5 collective-permute-start.19
  116.8 7.7 collective-permute-start.22
  120.1 5.5 collective-permute-start.23
  138.5 7.9 collective-permute-start.26
  141.8 5.7 collective-permute-start.27
  160.3 11.8 %collective-permute-start.30 = (f32[4,2,130,1]{2,0,3,1:T(4,128)S(1)}, f32[4,2,130,1]{2,0,3,1:T(4,128)S(1)}, u32[]{:S(2)}, u32[]{:S(2)}) collective-permute-start(f32[4,2,130,1]{2,0,3,1:T(4,128)S(1)} %copy.181), channel_id=1, source_target_pairs={{1,0},{2,1},{3,2},{5,4},{6,5},{7,6},{9,8},{10,9},{11,10},{13,12},{... | collective-permute-start | bytes 12488 | tf_op jit(solution)/shard_map/ppermute | solution.py:26
  163.7 9.6 %collective-permute-start.31 = (f32[4,2,130,1]{2,0,3,1:T(4,128)S(1)}, f32[4,2,130,1]{2,0,3,1:T(4,128)S(1)}, u32[]{:S(2)}, u32[]{:S(2)}) collective-permute-start(f32[4,2,130,1]{2,0,3,1:T(4,128)S(1)} %copy.183), channel_id=1, source_target_pairs={{0,1},{1,2},{2,3},{4,5},{5,6},{6,7},{8,9},{9,10},{10,11},{12,13},{... | collective-permute-start | bytes 12488 | tf_op jit(solution)/shard_map/ppermute | solution.py:24
  202.7 6.4 collective-permute-start.34
  204.9 5.5 collective-permute-start.35
  221.1 6.2 collective-permute-start.38
  223.4 5.5 collective-permute-start.39
  239.6 6.2 collective-permute-start.42
  241.9 5.5 collective-permute-start.43
  260.0 6.2 collective-permute-start.46
  262.3 5.5 collective-permute-start.47
  278.6 7.2 collective-permute-start.50
  281.9 5.5 collective-permute-start.51
  300.2 7.2 collective-permute-start.54
  303.5 5.5 collective-permute-start.55
  321.8 7.2 collective-permute-start.58
  325.1 5.5 collective-permute-start.59
  343.5 11.8 %collective-permute-start.62 = (f32[4,2,130,1]{2,0,3,1:T(4,128)S(1)}, f32[4,2,130,1]{2,0,3,1:T(4,128)S(1)}, u32[]{:S(2)}, u32[]{:S(2)}) collective-permute-start(f32[4,2,130,1]{2,0,3,1:T(4,128)S(1)} %copy.228), channel_id=1, source_target_pairs={{1,0},{2,1},{3,2},{5,4},{6,5},{7,6},{9,8},{10,9},{11,10},{13,12},{... | collective-permute-start | bytes 12488 | tf_op jit(solution)/shard_map/ppermute | solution.py:26
  346.8 9.6 %collective-permute-start.63 = (f32[4,2,130,1]{2,0,3,1:T(4,128)S(1)}, f32[4,2,130,1]{2,0,3,1:T(4,128)S(1)}, u32[]{:S(2)}, u32[]{:S(2)}) collective-permute-start(f32[4,2,130,1]{2,0,3,1:T(4,128)S(1)} %copy.230), channel_id=1, source_target_pairs={{0,1},{1,2},{2,3},{4,5},{5,6},{6,7},{8,9},{9,10},{10,11},{12,13},{... | collective-permute-start | bytes 12488 | tf_op jit(solution)/shard_map/ppermute | solution.py:24
  388.0 7.2 collective-permute-start.66
  410.3 8.8 collective-permute-start.70
  414.2 6.7 collective-permute-start.71
  436.0 7.2 collective-permute-start.74
  457.7 7.2 collective-permute-start.78
  479.8 7.2 collective-permute-start.82
  501.9 7.2 collective-permute-start.86
  505.2 5.5 collective-permute-start.87
  524.0 7.2 collective-permute-start.90
  546.3 11.9 %collective-permute-start.94 = (f32[4,2,130,1]{2,0,3,1:T(4,128)S(1)}, f32[4,2,130,1]{2,0,3,1:T(4,128)S(1)}, u32[]{:S(2)}, u32[]{:S(2)}) collective-permute-start(f32[4,2,130,1]{2,0,3,1:T(4,128)S(1)} %copy.279), channel_id=1, source_target_pairs={{1,0},{2,1},{3,2},{5,4},{6,5},{7,6},{9,8},{10,9},{11,10},{13,12},{... | collective-permute-start | bytes 12488 | tf_op jit(solution)/shard_map/ppermute | solution.py:26
  549.6 9.7 %collective-permute-start.95 = (f32[4,2,130,1]{2,0,3,1:T(4,128)S(1)}, f32[4,2,130,1]{2,0,3,1:T(4,128)S(1)}, u32[]{:S(2)}, u32[]{:S(2)}) collective-permute-start(f32[4,2,130,1]{2,0,3,1:T(4,128)S(1)} %copy.281), channel_id=1, source_target_pairs={{0,1},{1,2},{2,3},{4,5},{5,6},{6,7},{8,9},{9,10},{10,11},{12,13},{... | collective-permute-start | bytes 12488 | tf_op jit(solution)/shard_map/ppermute | solution.py:24
  592.1 8.4 collective-permute-start.98
  596.0 6.3 collective-permute-start.99
  616.6 8.4 collective-permute-start.102
  620.5 6.3 collective-permute-start.103
  641.4 8.6 collective-permute-start.106
  645.3 6.5 collective-permute-start.107
  666.3 8.4 collective-permute-start.110
  670.2 6.3 collective-permute-start.111
  691.1 8.4 collective-permute-start.114
  695.0 6.3 collective-permute-start.115
  715.8 8.4 collective-permute-start.118
  719.7 6.3 collective-permute-start.119
  730.5 9.0 collective-permute-start.120
  732.4 7.1 collective-permute-start.121
  742.8 21.8 %collective-permute-start.122 = (f32[4,2,130,1]{2,0,3,1:T(4,128)}, f32[4,2,130,1]{2,0,3,1:T(4,128)}, u32[]{:S(2)}, u32[]{:S(2)}) collective-permute-start(f32[4,2,130,1]{2,0,3,1:T(4,128)} %copy.339), channel_id=1, source_target_pairs={{1,0},{2,1},{3,2},{5,4},{6,5},{7,6},{9,8},{10,9},{11,10},{13,12},{... | collective-permute-start | bytes 12488 | tf_op jit(solution)/shard_map/ppermute | solution.py:26
  746.7 19.7 %collective-permute-start.123 = (f32[4,2,130,1]{2,0,3,1:T(4,128)}, f32[4,2,130,1]{2,0,3,1:T(4,128)}, u32[]{:S(2)}, u32[]{:S(2)}) collective-permute-start(f32[4,2,130,1]{2,0,3,1:T(4,128)} %copy.341), channel_id=1, source_target_pairs={{0,1},{1,2},{2,3},{4,5},{5,6},{6,7},{8,9},{9,10},{10,11},{12,13},{... | collective-permute-start | bytes 12488 | tf_op jit(solution)/shard_map/ppermute | solution.py:24
  771.6 27.9 %collective-permute-start.124 = (f32[4,2,1,128]{3,2,0,1:T(1,128)}, f32[4,2,1,128]{3,2,0,1:T(1,128)S(1)}, u32[]{:S(2)}, u32[]{:S(2)}) collective-permute-start(f32[4,2,1,128]{3,2,0,1:T(1,128)} %get-tuple-element.148), channel_id=1, source_target_pairs={{4,0},{8,4},{12,8},{5,1},{9,5},{13,9},{6,2},{10,6},{14,10},{7,3},{... | collective-permute-start | bytes 12296 | tf_op jit(solution)/shard_map/ppermute | solution.py:26
  773.6 25.9 %collective-permute-start.125 = (f32[4,2,1,128]{3,2,0,1:T(1,128)S(1)}, f32[4,2,1,128]{3,2,0,1:T(1,128)S(1)}, u32[]{:S(2)}, u32[]{:S(2)}) collective-permute-start(f32[4,2,1,128]{3,2,0,1:T(1,128)S(1)} %get-tuple-element.147), channel_id=1, source_target_pairs={{0,4},{4,8},{8,12},{1,5},{5,9},{9,13},{2,6},{6,10},{10,14},{3,7},{... | collective-permute-start | bytes 12296 | tf_op jit(solution)/shard_map/ppermute | solution.py:24
  803.8 34.2 %collective-permute-start.126 = (f32[4,2,130,1]{2,0,3,1:T(4,128)}, f32[4,2,130,1]{2,0,3,1:T(4,128)}, u32[]{:S(2)}, u32[]{:S(2)}) collective-permute-start(f32[4,2,130,1]{2,0,3,1:T(4,128)} %copy.343), channel_id=1, source_target_pairs={{1,0},{2,1},{3,2},{5,4},{6,5},{7,6},{9,8},{10,9},{11,10},{13,12},{... | collective-permute-start | bytes 12488 | tf_op jit(solution)/shard_map/ppermute | solution.py:26
  807.7 31.2 %collective-permute-start.127 = (f32[4,2,130,1]{2,0,3,1:T(4,128)}, f32[4,2,130,1]{2,0,3,1:T(4,128)}, u32[]{:S(2)}, u32[]{:S(2)}) collective-permute-start(f32[4,2,130,1]{2,0,3,1:T(4,128)} %copy.345), channel_id=1, source_target_pairs={{0,1},{1,2},{2,3},{4,5},{5,6},{6,7},{8,9},{9,10},{10,11},{12,13},{... | collective-permute-start | bytes 12488 | tf_op jit(solution)/shard_map/ppermute | solution.py:24
  (174 other events, 1769.7 us)
Sparse Core Ops, SparseCore 0:
  877.0 23.4 all-reduce.2
where the time goes:
time: 928 us; the launch traced here: 910 us
  starting transfers between devices  332 us (36%)
  other arithmetic  234 us (25%)
  local copies, waits for them, and re-layouts  205 us (22%)
  waiting for transfers between devices  103 us (11%)
  blocking collectives  18.5 us (2%)
  between operations  18 us (2%)
    ppermute x64, starting transfers between devices, with_halo(): lax.ppermute(tail, axis, [(i, (i + 1) % count) for i in range(ends)])  208 us
    ppermute x64, starting transfers between devices, with_halo(): lax.ppermute(head, axis, [((i + 1) % count, i) for i in range(ends)])  124 us
    ppermute x64, waiting for transfers between devices, with_halo(): lax.ppermute(tail, axis, [(i, (i + 1) % count) for i in range(ends)])  90.8 us
    reduce_sum x4, other arithmetic, per_device(): partial_image = jnp.sum(real_part, axis=0)  78.8 us
    slice x64, local copies, waits for them, and re-layouts, with_halo(): head = lax.slice_in_dim(cells, 0, width, axis=dim)  76.9 us
    concatenate x64, other arithmetic, with_halo(): jnp.concatenate([lax.ppermute(tail, axis, [(i, (i + 1) % count) for i in...  58.1 us
    slice x61, local copies, waits for them, and re-layouts, with_halo(): lax.slice_in_dim(cells, cells.shape[dim] - width, cells.shape[dim], axis=...  42.8 us
    ppermute x32, local copies, waits for them, and re-layouts, with_halo(): lax.ppermute(tail, axis, [(i, (i + 1) % count) for i in range(ends)])  38.7 us
  transfers between devices with their start and end apart: 129, of which 49 were waited for; matrix products, arithmetic and copies ran while one was open for 16% of the time, Pallas kernels for 0%

commit v1 on v0

v1 whole, which is shorter than its diff:
```python
import functools
import math

import jax
import jax.numpy as jnp
from jax import lax
from jax.experimental import pallas as pl
from jax.experimental.pallas import tpu as pltpu
from jax.sharding import PartitionSpec as P

ORDER = 8
LANES = 128
SUB = 8

lowest_freq = 2.0
highest_freq = 60.0
depth_interval = 0.01


class Plan:
    def __init__(self, wave_shape, depths):
        self.freqs, self.parts, self.rows, self.tile = wave_shape
        self.depths = depths
        self.halo = ORDER * depths
        self.cols = self.tile + 2 * self.halo
        self.span = LANES // self.freqs
        self.ways = self.cols // self.span
        self.tall = self.rows + 2 * self.halo
        assert self.tile == LANES and self.freqs * self.span == LANES
        assert self.halo == self.span and depths == self.freqs
        assert self.ways * self.span == self.cols and self.tall % SUB == 0


def term_weights(order):
    values = [1.0 / (term + 1) for term in range(order + 1)]
    whole = sum(values)
    return [value / whole for value in values]


def lane_iota(rows=SUB):
    return lax.broadcasted_iota(jnp.int32, (rows, LANES), 1)


def pick(block, index):
    return jnp.take_along_axis(block, index, axis=1, mode="promise_in_bounds")


def pack_kernel(plan, axis, src, first, second):
    even = lax.rem(lax.axis_index(axis), 2) == 0
    lanes = lane_iota()
    which = lanes // plan.span
    parts, rows = first.shape[0], first.shape[1]
    for part in range(parts):
        for row in range(0, rows, SUB):
            low = high = None
            for f in range(plan.freqs):
                block = src[f, part, row : row + SUB, :]
                shift = plan.span * f
                lo = pltpu.roll(block, shift, 1) if shift else block
                shift = (plan.span * f + plan.halo) % LANES
                hi = pltpu.roll(block, shift, 1) if shift else block
                low = lo if low is None else jnp.where(which == f, lo, low)
                high = hi if high is None else jnp.where(which == f, hi, high)
            first[part, row : row + SUB, :] = jnp.where(even, high, low)
            second[part, row : row + SUB, :] = jnp.where(even, low, high)


def assemble_kernel(plan, axis_y, axis_x, src, got_a, got_b, tile, send_a, send_b):
    even_y = lax.rem(lax.axis_index(axis_y), 2) == 0
    even_x = lax.rem(lax.axis_index(axis_x), 2) == 0
    lanes = lane_iota()
    which = lanes // plan.span
    within = lanes - which * plan.span
    parts, rows = got_a.shape[0], got_a.shape[1]
    for part in range(parts):
        for row in range(0, rows, SUB):
            here = slice(row, row + SUB)
            blocks = [src[f, part, here, :] for f in range(plan.freqs)]
            a, b = got_a[part, here, :], got_b[part, here, :]
            left = jnp.where(even_y, b, a)
            right = jnp.where(even_y, a, b)
            for v in range(plan.ways):
                column = plan.ways * within + v
                inner = column - plan.halo
                index = jnp.clip(inner, 0, LANES - 1)
                out = pick(blocks[0], index)
                for f in range(1, plan.freqs):
                    out = jnp.where(which == f, pick(blocks[f], index), out)
                index = which * plan.span + jnp.clip(column, 0, plan.halo - 1)
                out = jnp.where(inner < 0, pick(left, index), out)
                beyond = inner - plan.tile
                index = which * plan.span + jnp.clip(beyond, 0, plan.halo - 1)
                out = jnp.where(beyond >= 0, pick(right, index), out)
                tile[part, v, here, :] = out
    for part in range(parts):
        for v in range(plan.ways):
            for row in range(0, plan.halo, SUB):
                top = tile[part, v, row : row + SUB, :]
                start = rows - plan.halo + row
                low = tile[part, v, start : start + SUB, :]
                send_a[part, v, row : row + SUB, :] = jnp.where(even_x, low, top)
                send_b[part, v, row : row + SUB, :] = jnp.where(even_x, top, low)


def halved_trig(theta):
    t = theta * theta
    sine = 2.7557319e-06
    for c in (-1.9841270e-04, 8.3333333e-03, -1.6666667e-01, 1.0):
        sine = sine * t + c
    cosine = -2.7557319e-07
    for c in (2.4801587e-05, -1.3888889e-03, 4.1666667e-02, -0.5, 1.0):
        cosine = cosine * t + c
    return sine * theta, cosine


def migrate_kernel(plan, depth_list, order, axes, *refs):
    axis_f, axis_x, axis_y = axes
    first = depth_list[0] == 0
    last = depth_list[-1] == plan.depths - 1
    refs = list(refs)
    if first:
        core, core_a, core_b = refs[:3]
        vel, vel_a, vel_b = refs[3:6]
        refs = refs[6:]
    else:
        start, vel = refs[:2]
        refs = refs[2:]
    image, out = refs[:2]
    refs = refs[2:]
    if first:
        vel_out = None
        if not last:
            vel_out = refs[0]
            refs = refs[1:]
    hist = refs[0]
    halo, rows, ways, span = plan.halo, plan.rows, plan.ways, plan.span
    pad = SUB
    tiles = plan.tall // SUB
    gx, gy = lax.axis_index(axis_x), lax.axis_index(axis_y)
    even_x = lax.rem(gx, 2) == 0
    lanes = lane_iota()
    which = lanes // span
    within = lanes - which * span
    subl = lax.broadcasted_iota(jnp.int32, (SUB, LANES), 0)

    left_col, right_col = halo - 1, halo + plan.tile
    edge_left = (gy == 0) & (within == left_col // ways)
    edge_right = (gy == lax.axis_size(axis_y) - 1) & (within == right_col // ways)
    edge_top = (gx == 0) & (subl == (halo - 1) % SUB)
    edge_low = (gx == lax.axis_size(axis_x) - 1) & (subl == (halo + rows) % SUB)
    top_tile, low_tile = (halo - 1) // SUB, (halo + rows) // SUB

    def grid_edges(value, v, t):
        if v == left_col % ways:
            value = jnp.where(edge_left, 0.0, value)
        if v == right_col % ways:
            value = jnp.where(edge_right, 0.0, value)
        if t == top_tile:
            value = jnp.where(edge_top, 0.0, value)
        if t == low_tile:
            value = jnp.where(edge_low, 0.0, value)
        return value

    if first:
        for part in range(plan.parts):
            for v in range(ways):
                for row in range(0, halo, SUB):
                    a = core_a[part, v, row : row + SUB, :]
                    b = core_b[part, v, row : row + SUB, :]
                    hist[0, part, v, pad + row : pad + row + SUB, :] = jnp.where(even_x, b, a)
                    at = pad + halo + rows + row
                    hist[0, part, v, at : at + SUB, :] = jnp.where(even_x, a, b)
                for row in range(0, rows, SUB):
                    at = pad + halo + row
                    hist[0, part, v, at : at + SUB, :] = core[part, v, row : row + SUB, :]
    else:
        lead = SUB * depth_list[0]
        for part in range(plan.parts):
            for v in range(ways):
                for row in range(lead, plan.tall - lead, SUB):
                    hist[0, part, v, pad + row : pad + row + SUB, :] = start[
                        part, v, row - lead : row - lead + SUB, :
                    ]

    def velocity_at(v, t):
        row = t * SUB
        if not first:
            lead = SUB * (depth_list[0] + 1)
            return vel[v, row - lead : row - lead + SUB, :]
        if row < halo:
            a, b = vel_a[0, v, row : row + SUB, :], vel_b[0, v, row : row + SUB, :]
            return jnp.where(even_x, b, a)
        if row < halo + rows:
            return vel[0, v, row - halo : row - halo + SUB, :]
        row = row - halo - rows
        a, b = vel_a[0, v, row : row + SUB, :], vel_b[0, v, row : row + SUB, :]
        return jnp.where(even_x, a, b)

    weights = term_weights(order)
    count = plan.freqs
    total = count * lax.axis_size(axis_f)
    freq = (lax.axis_index(axis_f) * count + which).astype(jnp.float32)
    angular = (2.0 * math.pi) * (
        lowest_freq + (highest_freq - lowest_freq) * (freq + 0.5) / total
    )
    rate = angular * (depth_interval / (order + 1))

    def apply(n, t, opening):
        for part in range(plan.parts):
            at = pad + t * SUB
            double, across = [], []
            for v in range(ways):
                mid = hist[n - 1, part, v, at : at + SUB, :]
                up = hist[n - 1, part, v, at - 1 : at - 1 + SUB, :]
                down = hist[n - 1, part, v, at + 1 : at + 1 + SUB, :]
                two = mid if opening else mid + mid
                double.append(two)
                across.append((mid + mid) + (up + down))
            wrap_low = pltpu.roll(across[-1], 1, 1)
            wrap_high = pltpu.roll(across[0], LANES - 1, 1)
            line = [wrap_low] + across + [wrap_high]
            pairs = [line[i] + line[i + 1] for i in range(ways + 1)]
            for v in range(ways):
                total_sum = pairs[v] + pairs[v + 1]
                if opening:
                    value = 0.125 * total_sum - double[v]
                else:
                    before = hist[n - 2, part, v, at : at + SUB, :]
                    value = (0.25 * total_sum - double[v]) - before
                hist[n, part, v, at : at + SUB, :] = grid_edges(value, v, t)

    for slot, depth in enumerate(depth_list):
        for t in range(depth, tiles - depth):
            apply(1, t, True)

        def step(n, carry):
            for t in range(depth, tiles - depth):
                apply(n, t, False)
            return carry

        lax.fori_loop(2, order + 1, step, 0)
        final = depth == plan.depths - 1
        spread = depth * span + within
        for t in range(depth + 1, tiles - depth - 1):
            at = pad + t * SUB
            fresh = []
            for v in range(ways):
                speed = pick(velocity_at(v, t), spread)
                speed = jnp.where(speed > 0.0, speed, 1.0)
                sine, cosine = halved_trig(rate / speed)
                twice = cosine + cosine
                ends = []
                for part in range(plan.parts):
                    near = weights[order] * hist[order, part, v, at : at + SUB, :]
                    far = None
                    for n in range(order - 1, -1, -1):
                        value = weights[n] * hist[n, part, v, at : at + SUB, :] + twice * near
                        if far is not None:
                            value = value - far
                        near, far = value, near
                    ends.append((near, far))
                (real, real_far), (imag, imag_far) = ends
                fresh.append(
                    (
                        cosine * real - sine * imag - real_far,
                        sine * real + cosine * imag - imag_far,
                    )
                )
            inside = halo <= t * SUB < halo + rows
            home = t * SUB - halo
            if inside:
                natural = lanes + halo
                source = natural // ways
                turn = natural - source * ways
                tally = None
                for v in range(ways):
                    fold = fresh[v][0]
                    width = LANES // 2
                    while width >= span:
                        fold = fold + pltpu.roll(fold, width, 1)
                        width //= 2
                    fold = pick(fold, source)
                    tally = fold if tally is None else jnp.where(turn == v, fold, tally)
                image[slot, home : home + SUB, :] = tally
            if final:
                for part in range(plan.parts):
                    for f in range(plan.freqs):
                        value = None
                        for v in range(ways):
                            moved = pick(fresh[v][part], f * span + source)
                            value = moved if value is None else jnp.where(turn == v, moved, value)
                        out[f, part, home : home + SUB, :] = value
            elif depth == depth_list[-1]:
                lead = SUB * (depth + 1)
                row = t * SUB - lead
                for v in range(ways):
                    for part in range(plan.parts):
                        out[part, v, row : row + SUB, :] = fresh[v][part]
            else:
                for v in range(ways):
                    for part in range(plan.parts):
                        hist[0, part, v, at : at + SUB, :] = fresh[v][part]
    if first and not last:
        lead = SUB * (depth_list[-1] + 2)
        for v in range(ways):
            for row in range(lead, plan.tall - lead, SUB):
                vel_out[v, row - lead : row - lead + SUB, :] = velocity_at(v, row // SUB)


def swap(value, axis, odd):
    count = lax.axis_size(axis)
    pairs = []
    for i in range(odd, count - 1, 2):
        pairs += [(i, i + 1), (i + 1, i)]
    if not pairs:
        return jnp.zeros_like(value)
    return lax.ppermute(value, axis, pairs)


def gather_rows(value, axis):
    count, index = lax.axis_size(axis), lax.axis_index(axis)
    assert count & (count - 1) == 0
    width = 1
    while width < count:
        got = lax.ppermute(value, axis, [(i, i ^ width) for i in range(count)])
        low = (index // width) % 2 == 0
        value = jnp.concatenate([jnp.where(low, value, got), jnp.where(low, got, value)], axis=1)
        width *= 2
    return value


def sum_over(value, axis):
    count = lax.axis_size(axis)
    width = 1
    while width < count:
        value = value + lax.ppermute(value, axis, [(i, i ^ width) for i in range(count)])
        width *= 2
    return value


VMEM = pl.BlockSpec(memory_space=pltpu.VMEM)


def call(kernel, ins, outs, scratch=(), flops=0, name=None):
    moved = sum(4 * math.prod(x.shape) for x in ins) + sum(4 * math.prod(s) for s in outs)
    return pl.pallas_call(
        kernel,
        out_shape=[jax.ShapeDtypeStruct(s, jnp.float32) for s in outs],
        in_specs=[VMEM] * len(ins),
        out_specs=[VMEM] * len(outs),
        scratch_shapes=list(scratch),
        cost_estimate=pl.CostEstimate(flops=flops, bytes_accessed=moved, transcendentals=0),
        name=name,
    )(*ins)


def extended(plan, source):
    parts, rows = source.shape[1], source.shape[2]
    edge = (parts, rows, LANES)
    first, second = call(
        functools.partial(pack_kernel, plan, "gy"), [source], [edge, edge], name="pack"
    )
    got_a, got_b = swap(first, "gy", 0), swap(second, "gy", 1)
    slab = (parts, plan.ways, plan.halo, LANES)
    tile, send_a, send_b = call(
        functools.partial(assemble_kernel, plan, "gy", "gx"),
        [source, got_a, got_b],
        [(parts, plan.ways, rows, LANES), slab, slab],
        name="assemble",
    )
    return tile, swap(send_a, "gx", 0), swap(send_b, "gx", 1)


def per_device(wavefield, velocity):
    order = ORDER
    plan = Plan(wavefield.shape, velocity.shape[0])
    axes = ("freq", "gx", "gy")
    freq_total = plan.freqs * lax.axis_size("freq")
    speeds = gather_rows(velocity, "freq")[:, None]
    wave = extended(plan, wavefield)
    slabs = extended(plan, speeds)
    depths = list(range(plan.depths))
    head, tail = depths[:-1], depths[-1:]
    kept = plan.tall - 2 * SUB * len(head)
    need = plan.tall - 2 * SUB * (len(head) + 1)
    hist = pltpu.VMEM((order + 1, plan.parts, plan.ways, plan.tall + 2 * SUB, LANES), jnp.float32)
    square = (plan.rows, plan.tile)
    image_head, middle, speed_mid = call(
        functools.partial(migrate_kernel, plan, head, order, axes),
        [*wave, *slabs],
        [(len(head),) + square, (plan.parts, plan.ways, kept, LANES), (plan.ways, need, LANES)],
        [hist],
        flops=30_000_000,
        name="head",
    )
    image_tail, last = call(
        functools.partial(migrate_kernel, plan, tail, order, axes),
        [middle, speed_mid],
        [(len(tail),) + square, wavefield.shape],
        [hist],
        flops=30_000_000,
        name="tail",
    )
    scale = 1.0 / math.sqrt(freq_total)
    image = jnp.concatenate([sum_over(image_head, "freq"), sum_over(image_tail, "freq")]) * scale
    return image, last


def solution(mesh):
    placed = (P("freq", None, "gx", "gy"), P(None, ("gx", "freq"), "gy"))
    return jax.shard_map(
        per_device,
        mesh=mesh,
        in_specs=placed,
        out_specs=(P(None, "gx", "gy"), P("freq", None, "gx", "gy")),
        check_vma=False,
    )
```

time: 928 us -> 180 us (0.19); the launches traced: 910 us -> 180 us
  starting transfers between devices: 332 us -> 13.9 us
  other arithmetic: 234 us -> 2.35 us
  local copies, waits for them, and re-layouts: 205 us -> 2.04 us
  Pallas kernels: 0 us -> 145 us
  waiting for transfers between devices: 103 us -> 15.7 us
  blocking collectives: 18.5 us -> 0 us
  between operations: 18 us -> 0.76 us
    ppermute x128 -> x11, starting transfers between devices: 332 us -> 13.9 us  [the longest x8 10.3 us: swap(): return lax.ppermute(value, axis, pairs)]
    pallas_call x0 -> x6, Pallas kernels: none -> 145 us  [call(): pl.pallas_call(kernel, out_shape=[jax.ShapeDtypeStruct(s, jnp.float32) fo...]
    slice x126 -> x0, local copies, waits for them, and re-layouts: 120 us -> none  [the longest x64 76.9 us: with_halo(): head = lax.slice_in_dim(cells, 0, width, axis=dim)]
    reduce_sum x4 -> x0, other arithmetic: 78.8 us -> none  [per_device(): partial_image = jnp.sum(real_part, axis=0)]
    ppermute x128 -> x11, waiting for transfers between devices: 91 us -> 15.7 us  [the longest x8 11.8 us: swap(): return lax.ppermute(value, axis, pairs)]
    add x12 -> x2, other arithmetic: 75.5 us -> 0.88 us  [sum_over(): value + lax.ppermute(value, axis, [(i, i ^ width) for i in range(count)])]
    ppermute x64 -> x0, local copies, waits for them, and re-layouts: 73.2 us -> none  [the longest x32 38.7 us: with_halo(): lax.ppermute(tail, axis, [(i, (i + 1) % count) for i in range(ends)])]
    concatenate x64 -> x0, other arithmetic: 58.1 us -> none  [with_halo(): jnp.concatenate([lax.ppermute(tail, axis, [(i, (i + 1) % count) for i in...]
  transfers between devices with their start and end apart: 129 -> 11, of which waited for: 49 -> 6; matrix products, arithmetic and copies ran while one was open for 16% -> 1% of each run, Pallas kernels for 0% -> 24%
where the time goes in v1:
time: 180 us
  Pallas kernels  145 us (81%)
  waiting for transfers between devices  15.7 us (9%)
  starting transfers between devices  13.9 us (8%)
  other arithmetic  2.35 us (1%)
  local copies, waits for them, and re-layouts  2.04 us (1%)
    pallas_call x6, Pallas kernels, call(): pl.pallas_call(kernel, out_shape=[jax.ShapeDtypeStruct(s, jnp.float32) fo...  145 us
    ppermute x8, waiting for transfers between devices, swap(): return lax.ppermute(value, axis, pairs)  11.8 us
    ppermute x8, starting transfers between devices, swap(): return lax.ppermute(value, axis, pairs)  10.3 us
    ppermute x2, waiting for transfers between devices, sum_over(): lax.ppermute(value, axis, [(i, i ^ width) for i in range(count)])  3.94 us
  transfers between devices with their start and end apart: 11, of which 6 were waited for; matrix products, arithmetic and copies ran while one was open for 1% of the time, Pallas kernels for 24%

profile of v1, /device:TPU:20, one launch (start us, length us, event | category | flops | bytes accessed | tf_op | source)
XLA Modules:
  0.0 180.0 jit_solution(8682759179153853613)
XLA Ops:
  0.6 0.0 copy-start.3
  0.6 2.0 %pack.2 = (f32[2,128,128]{2,1,0:T(8,128)}, f32[2,128,128]{2,1,0:T(8,128)}) custom-call(f32[4,2,128,128]{3,2,1,0:T(8,128)} %src.3), custom_call_target="tpu_custom_call" | custom-call | bytes 786432 | tf_op jit(solution)/shard_map/pack/pallas_call | solution.py:346
  2.7 1.6 collective-permute-start
  4.3 1.9 %collective-permute-start.1 = (f32[2,128,128]{2,1,0:T(8,128)}, f32[2,128,128]{2,1,0:T(8,128)S(1)}, u32[]{:S(2)}, u32[]{:S(2)}) collective-permute-start(f32[2,128,128]{2,1,0:T(8,128)} %get-tuple-element.18), channel_id=1, source_target_pairs={{1,2},{2,1},{5,6},{6,5},{9,10},{10,9},{13,14},{14,13},{17,18},{18,... | collective-permute-start | bytes 393224 | tf_op jit(solution)/shard_map/ppermute | solution.py:317
  6.2 0.0 copy-done.3
  6.2 1.6 collective-permute-start.4
  7.7 0.4 collective-permute-done.got_a
  8.1 0.0 copy-start.4
  8.1 3.2 %collective-permute-done.1.got_b = f32[2,128,128]{2,1,0:T(8,128)S(1)} collective-permute-done((f32[2,128,128]{2,1,0:T(8,128)}, f32[2,128,128]{2,1,0:T(8,128)S(1)}, u32[]{:S(2)}, u32[]{:S(2)}) %collective-permute-start.1) | collective-permute-done | bytes 131104 | tf_op jit(solution)/shard_map/ppermute | solution.py:317
  11.3 0.0 copy-done.4
  11.3 0.0 copy-start.5
  11.3 0.7 copy-done.5
  12.0 4.7 %assemble.2 = (f32[2,6,128,128]{3,2,1,0:T(8,128)}, f32[2,6,32,128]{3,2,1,0:T(8,128)}, f32[2,6,32,128]{3,2,1,0:T(8,128)}) custom-call(f32[4,2,128,128]{3,2,1,0:T(8,128)} %src.3, f32[2,128,128]{2,1,0:T(8,128)} %copy-done.4, f32[2,128,128]{2,1,0:T(8,128)} %copy-done.5), custom_call_target="tpu_custom_call" | custom-call | bytes 1966080 | tf_op jit(solution)/shard_map/assemble/pallas_call | solution.py:346
  16.6 0.0 collective-permute-start.2
  16.6 2.5 %collective-permute-start.3 = (f32[2,6,32,128]{3,2,1,0:T(8,128)}, f32[2,6,32,128]{3,2,1,0:T(8,128)S(1)}, u32[]{:S(2)}, u32[]{:S(2)}) collective-permute-start(f32[2,6,32,128]{3,2,1,0:T(8,128)} %get-tuple-element.21), channel_id=1, source_target_pairs={{4,8},{8,4},{5,9},{9,5},{6,10},{10,6},{7,11},{11,7},{20,24},{24,20... | collective-permute-start | bytes 589832 | tf_op jit(solution)/shard_map/ppermute | solution.py:317
  19.2 0.0 collective-permute-done.4
  19.2 0.7 maximum_bitcast_fusion.src
  19.9 1.8 pack.3
  21.7 0.0 collective-permute-start.5
  21.7 2.2 %collective-permute-start.6 = (f32[1,128,128]{2,1,0:T(8,128)}, f32[1,128,128]{2,1,0:T(8,128)S(1)}, u32[]{:S(2)}, u32[]{:S(2)}) collective-permute-start(f32[1,128,128]{2,1,0:T(8,128)} %get-tuple-element.23), channel_id=1, source_target_pairs={{1,2},{2,1},{5,6},{6,5},{9,10},{10,9},{13,14},{14,13},{17,18},{18,... | collective-permute-start | bytes 196616 | tf_op jit(solution)/shard_map/ppermute | solution.py:317
  23.9 2.3 %collective-permute-done.5.got_a = f32[1,128,128]{2,1,0:T(8,128)S(1)} collective-permute-done((f32[1,128,128]{2,1,0:T(8,128)}, f32[1,128,128]{2,1,0:T(8,128)S(1)}, u32[]{:S(2)}, u32[]{:S(2)}) %collective-permute-start.5) | collective-permute-done | bytes 65568 | tf_op jit(solution)/shard_map/ppermute | solution.py:317
  26.2 0.0 copy-start.8
  26.2 1.9 %collective-permute-done.6.got_b = f32[1,128,128]{2,1,0:T(8,128)S(1)} collective-permute-done((f32[1,128,128]{2,1,0:T(8,128)}, f32[1,128,128]{2,1,0:T(8,128)S(1)}, u32[]{:S(2)}, u32[]{:S(2)}) %collective-permute-start.6) | collective-permute-done | bytes 65568 | tf_op jit(solution)/shard_map/ppermute | solution.py:317
  28.0 0.0 copy-done.8
  28.0 0.0 copy-start.9
  28.1 0.6 copy-done.9
  28.7 3.1 %assemble.3 = (f32[1,6,128,128]{3,2,1,0:T(8,128)}, f32[1,6,32,128]{3,2,1,0:T(8,128)}, f32[1,6,32,128]{3,2,1,0:T(8,128)}) custom-call(f32[4,1,128,128]{3,2,1,0:T(8,128)} %maximum_bitcast_fusion.src, f32[1,128,128]{2,1,0:T(8,128)} %copy-done.8, f32[1,128,128]{2,1,0:T(8,128)} %copy-done.9), custom_call_target="tpu_custom_call" | custom-call | bytes 983040 | tf_op jit(solution)/shard_map/assemble/pallas_call | solution.py:346
  31.8 0.0 collective-permute-start.7
  31.8 2.1 %collective-permute-start.8 = (f32[1,6,32,128]{3,2,1,0:T(8,128)}, f32[1,6,32,128]{3,2,1,0:T(8,128)S(1)}, u32[]{:S(2)}, u32[]{:S(2)}) collective-permute-start(f32[1,6,32,128]{3,2,1,0:T(8,128)} %get-tuple-element.26), channel_id=1, source_target_pairs={{4,8},{8,4},{5,9},{9,5},{6,10},{10,6},{7,11},{11,7},{20,24},{24,20... | collective-permute-start | bytes 294920 | tf_op jit(solution)/shard_map/ppermute | solution.py:317
  33.9 0.0 collective-permute-done.7.refs_4_
  33.9 0.0 copy-start.6
  33.9 4.0 %collective-permute-done.8.refs_5_ = f32[1,6,32,128]{3,2,1,0:T(8,128)S(1)} collective-permute-done((f32[1,6,32,128]{3,2,1,0:T(8,128)}, f32[1,6,32,128]{3,2,1,0:T(8,128)S(1)}, u32[]{:S(2)}, u32[]{:S(2)}) %collective-permute-start.8) | collective-permute-done | bytes 98336 | tf_op jit(solution)/shard_map/ppermute | solution.py:317
  37.9 0.0 copy-start.7
  37.9 0.0 collective-permute-done.2.refs_1_
  37.9 0.0 copy-start
  37.9 0.0 collective-permute-done.3.refs_2_
  37.9 0.0 copy-start.1
  37.9 0.0 copy-done.6
  37.9 0.6 copy-done.7
  38.5 0.1 copy-done
  38.6 0.1 copy-done.1
  38.7 99.5 %head.1 = (f32[3,128,128]{2,1,0:T(8,128)}, f32[2,6,144,128]{3,2,1,0:T(8,128)}, f32[6,128,128]{2,1,0:T(8,128)}) custom-call(f32[2,6,128,128]{3,2,1,0:T(8,128)} %get-tuple-element.19.refs_0_, f32[2,6,32,128]{3,2,1,0:T(8,128)} %copy-done, f32[2,6,32,128]{3,2,1,0:T(8,128)} %copy-done.1, f32[1,6,128,128]{3,2,1,0:T(8,128)} %get-tuple-element.24.refs_3_, ...), custom_call_target="tpu_custom_call" | custom-call | flops 30000000 | bytes 3244032 | tf_op jit(solution)/shard_map/head/pallas_call | solution.py:346
  138.2 1.5 collective-permute-start.9
  139.7 34.2 %tail.1 = (f32[1,128,128]{2,1,0:T(8,128)}, f32[4,2,128,128]{3,2,1,0:T(8,128)}) custom-call(f32[2,6,144,128]{3,2,1,0:T(8,128)} %get-tuple-element.28.refs_0_, f32[6,128,128]{2,1,0:T(8,128)} %get-tuple-element.29.refs_1_), custom_call_target="tpu_custom_call" | custom-call | flops 30000000 | bytes 1867776 | tf_op jit(solution)/shard_map/tail/pallas_call | solution.py:346
  173.9 0.0 copy-start.2
  173.9 0.5 collective-permute-start.10
  174.4 3.9 %collective-permute-done.10 = f32[1,128,128]{2,1,0:T(8,128)S(1)} collective-permute-done((f32[1,128,128]{2,1,0:T(8,128)}, f32[1,128,128]{2,1,0:T(8,128)S(1)}, u32[]{:S(2)}, u32[]{:S(2)}) %collective-permute-start.10) | collective-permute-done | bytes 65568 | tf_op jit(solution)/shard_map/ppermute | solution.py:336
  178.3 0.9 add.13
  179.2 0.0 collective-permute-done.9
  179.2 0.0 copy-done.2
  179.2 0.7 maximum_multiply_fusion
  (2 shorter events, 0.1 us)
Async XLA Ops:
  0.6 5.6 %copy-start.3 = (f32[4,64,128]{2,1,0:T(8,128)S(1)}, f32[4,64,128]{2,1,0:T(8,128)}, u32[]{:S(2)}) copy-start(f32[4,64,128]{2,1,0:T(8,128)} %param.3) | copy-start | bytes 393220
  2.7 5.4 %collective-permute-start = (f32[2,128,128]{2,1,0:T(8,128)}, f32[2,128,128]{2,1,0:T(8,128)S(1)}, u32[]{:S(2)}, u32[]{:S(2)}) collective-permute-start(f32[2,128,128]{2,1,0:T(8,128)} %get-tuple-element.17), channel_id=1, source_target_pairs={{0,1},{1,0},{2,3},{3,2},{4,5},{5,4},{6,7},{7,6},{8,9},{9,8},{10,11... | collective-permute-start | bytes 393224 | tf_op jit(solution)/shard_map/ppermute | solution.py:317
  4.3 7.1 %collective-permute-start.1 = (f32[2,128,128]{2,1,0:T(8,128)}, f32[2,128,128]{2,1,0:T(8,128)S(1)}, u32[]{:S(2)}, u32[]{:S(2)}) collective-permute-start(f32[2,128,128]{2,1,0:T(8,128)} %get-tuple-element.18), channel_id=1, source_target_pairs={{1,2},{2,1},{5,6},{6,5},{9,10},{10,9},{13,14},{14,13},{17,18},{18,... | collective-permute-start | bytes 393224 | tf_op jit(solution)/shard_map/ppermute | solution.py:317
  6.2 13.0 %collective-permute-start.4 = (f32[4,64,128]{2,1,0:T(8,128)S(1)}, f32[4,64,128]{2,1,0:T(8,128)S(1)}, u32[]{:S(2)}, u32[]{:S(2)}) collective-permute-start(f32[4,64,128]{2,1,0:T(8,128)S(1)} %copy-done.3), channel_id=1, source_target_pairs={{0,16},{16,0},{1,17},{17,1},{2,18},{18,2},{3,19},{19,3},{4,20},{20... | collective-permute-start | bytes 393224 | tf_op jit(solution)/shard_map/ppermute | solution.py:325
  8.1 3.2 %copy-start.4 = (f32[2,128,128]{2,1,0:T(8,128)}, f32[2,128,128]{2,1,0:T(8,128)S(1)}, u32[]{:S(2)}) copy-start(f32[2,128,128]{2,1,0:T(8,128)S(1)} %collective-permute-done.got_a) | copy-start | bytes 393220
  11.3 0.7 copy-start.5
  16.6 21.3 %collective-permute-start.2 = (f32[2,6,32,128]{3,2,1,0:T(8,128)}, f32[2,6,32,128]{3,2,1,0:T(8,128)S(1)}, u32[]{:S(2)}, u32[]{:S(2)}) collective-permute-start(f32[2,6,32,128]{3,2,1,0:T(8,128)} %get-tuple-element.20), channel_id=1, source_target_pairs={{0,4},{4,0},{8,12},{12,8},{1,5},{5,1},{9,13},{13,9},{2,6},{6,2},{1... | collective-permute-start | bytes 589832 | tf_op jit(solution)/shard_map/ppermute | solution.py:317
  16.6 21.3 %collective-permute-start.3 = (f32[2,6,32,128]{3,2,1,0:T(8,128)}, f32[2,6,32,128]{3,2,1,0:T(8,128)S(1)}, u32[]{:S(2)}, u32[]{:S(2)}) collective-permute-start(f32[2,6,32,128]{3,2,1,0:T(8,128)} %get-tuple-element.21), channel_id=1, source_target_pairs={{4,8},{8,4},{5,9},{9,5},{6,10},{10,6},{7,11},{11,7},{20,24},{24,20... | collective-permute-start | bytes 589832 | tf_op jit(solution)/shard_map/ppermute | solution.py:317
  21.7 4.5 %collective-permute-start.5 = (f32[1,128,128]{2,1,0:T(8,128)}, f32[1,128,128]{2,1,0:T(8,128)S(1)}, u32[]{:S(2)}, u32[]{:S(2)}) collective-permute-start(f32[1,128,128]{2,1,0:T(8,128)} %get-tuple-element.22), channel_id=1, source_target_pairs={{0,1},{1,0},{2,3},{3,2},{4,5},{5,4},{6,7},{7,6},{8,9},{9,8},{10,11... | collective-permute-start | bytes 196616 | tf_op jit(solution)/shard_map/ppermute | solution.py:317
  21.7 6.4 %collective-permute-start.6 = (f32[1,128,128]{2,1,0:T(8,128)}, f32[1,128,128]{2,1,0:T(8,128)S(1)}, u32[]{:S(2)}, u32[]{:S(2)}) collective-permute-start(f32[1,128,128]{2,1,0:T(8,128)} %get-tuple-element.23), channel_id=1, source_target_pairs={{1,2},{2,1},{5,6},{6,5},{9,10},{10,9},{13,14},{14,13},{17,18},{18,... | collective-permute-start | bytes 196616 | tf_op jit(solution)/shard_map/ppermute | solution.py:317
  26.2 1.9 %copy-start.8 = (f32[1,128,128]{2,1,0:T(8,128)}, f32[1,128,128]{2,1,0:T(8,128)S(1)}, u32[]{:S(2)}) copy-start(f32[1,128,128]{2,1,0:T(8,128)S(1)} %collective-permute-done.5.got_a) | copy-start | bytes 196612
  28.0 0.6 copy-start.9
  31.8 2.1 %collective-permute-start.7 = (f32[1,6,32,128]{3,2,1,0:T(8,128)}, f32[1,6,32,128]{3,2,1,0:T(8,128)S(1)}, u32[]{:S(2)}, u32[]{:S(2)}) collective-permute-start(f32[1,6,32,128]{3,2,1,0:T(8,128)} %get-tuple-element.25), channel_id=1, source_target_pairs={{0,4},{4,0},{8,12},{12,8},{1,5},{5,1},{9,13},{13,9},{2,6},{6,2},{1... | collective-permute-start | bytes 294920 | tf_op jit(solution)/shard_map/ppermute | solution.py:317
  31.8 6.1 %collective-permute-start.8 = (f32[1,6,32,128]{3,2,1,0:T(8,128)}, f32[1,6,32,128]{3,2,1,0:T(8,128)S(1)}, u32[]{:S(2)}, u32[]{:S(2)}) collective-permute-start(f32[1,6,32,128]{3,2,1,0:T(8,128)} %get-tuple-element.26), channel_id=1, source_target_pairs={{4,8},{8,4},{5,9},{9,5},{6,10},{10,6},{7,11},{11,7},{20,24},{24,20... | collective-permute-start | bytes 294920 | tf_op jit(solution)/shard_map/ppermute | solution.py:317
  33.9 4.1 %copy-start.6 = (f32[1,6,32,128]{3,2,1,0:T(8,128)}, f32[1,6,32,128]{3,2,1,0:T(8,128)S(1)}, u32[]{:S(2)}) copy-start(f32[1,6,32,128]{3,2,1,0:T(8,128)S(1)} %collective-permute-done.7.refs_4_) | copy-start | bytes 294916
  37.9 0.6 copy-start.7
  37.9 0.7 copy-start
  37.9 0.8 copy-start.1
  138.2 41.0 %collective-permute-start.9 = (f32[3,128,128]{2,1,0:T(8,128)}, f32[3,128,128]{2,1,0:T(8,128)S(1)}, u32[]{:S(2)}, u32[]{:S(2)}) collective-permute-start(f32[3,128,128]{2,1,0:T(8,128)} %get-tuple-element.27), channel_id=1, source_target_pairs={{0,16},{16,0},{1,17},{17,1},{2,18},{18,2},{3,19},{19,3},{4,20},{20... | collective-permute-start | bytes 589832 | tf_op jit(solution)/shard_map/ppermute | solution.py:336
  173.9 5.3 %copy-start.2 = (f32[3,128,128]{2,1,0:T(8,128)S(1)}, f32[3,128,128]{2,1,0:T(8,128)}, u32[]{:S(2)}) copy-start(f32[3,128,128]{2,1,0:T(8,128)} %get-tuple-element.27) | copy-start | bytes 589828
  173.9 4.5 %collective-permute-start.10 = (f32[1,128,128]{2,1,0:T(8,128)}, f32[1,128,128]{2,1,0:T(8,128)S(1)}, u32[]{:S(2)}, u32[]{:S(2)}) collective-permute-start(f32[1,128,128]{2,1,0:T(8,128)} %get-tuple-element.30), channel_id=1, source_target_pairs={{0,16},{16,0},{1,17},{17,1},{2,18},{18,2},{3,19},{19,3},{4,20},{20... | collective-permute-start | bytes 196616 | tf_op jit(solution)/shard_map/ppermute | solution.py:336

commit v2 on v1

v2 whole, which is shorter than its diff:
```python
import functools
import itertools
import math

import jax
import jax.numpy as jnp
from jax import lax
from jax.experimental import pallas as pl
from jax.experimental.pallas import tpu as pltpu
from jax.sharding import PartitionSpec as P

ORDER = 8
LANES = 128
SUB = 8

lowest_freq = 2.0
highest_freq = 60.0
depth_interval = 0.01


class Plan:
    def __init__(self, wave_shape, depths):
        self.freqs, self.parts, self.rows, self.tile = wave_shape
        self.depths = depths
        self.halo = ORDER * depths
        self.cols = self.tile + 2 * self.halo
        self.span = LANES // self.freqs
        self.ways = self.cols // self.span
        self.tall = self.rows + 2 * self.halo
        assert self.tile == LANES and self.freqs * self.span == LANES
        assert self.halo == self.span and depths == self.freqs
        assert self.ways * self.span == self.cols and self.tall % SUB == 0
        assert (self.halo + self.tile) % self.ways != 0
        self.offsets = self.find_offsets()

    def find_offsets(self):
        for offsets in itertools.product(range(LANES), repeat=self.freqs - 1):
            offsets = (0,) + offsets
            good = True
            for v in range(self.ways):
                seen = set()
                for offset in offsets:
                    first = (v - self.halo) % self.ways
                    mine = {(y + offset) % LANES for y in range(first, self.tile, self.ways)}
                    good = good and not (seen & mine)
                    seen |= mine
            if good:
                return offsets
        raise ValueError("no offsets")


def term_weights(order):
    values = [1.0 / (term + 1) for term in range(order + 1)]
    whole = sum(values)
    return [value / whole for value in values]


def lane_iota(rows=SUB):
    return lax.broadcasted_iota(jnp.int32, (rows, LANES), 1)


def pick(block, index):
    return jnp.take_along_axis(block, index, axis=1, mode="promise_in_bounds")


def turn(value, shift):
    return pltpu.roll(value, shift % LANES, 1) if shift % LANES else value


def pack_edges(plan, even, which, blocks):
    low = high = None
    for f, block in enumerate(blocks):
        lo = turn(block, plan.span * f)
        hi = turn(block, plan.span * f + plan.halo)
        low = lo if low is None else jnp.where(which == f, lo, low)
        high = hi if high is None else jnp.where(which == f, hi, high)
    return jnp.where(even, high, low), jnp.where(even, low, high)


def pack_kernel(plan, axis, src, first, second):
    even = lax.rem(lax.axis_index(axis), 2) == 0
    which = lane_iota() // plan.span
    parts, rows = first.shape[0], first.shape[1]
    for part in range(parts):
        for row in range(0, rows, SUB):
            here = slice(row, row + SUB)
            blocks = [src[f, part, here, :] for f in range(plan.freqs)]
            first[part, here, :], second[part, here, :] = pack_edges(plan, even, which, blocks)


def pack_slowness_kernel(plan, axis, axis_f, count, *refs):
    pieces, (natural, first, second) = refs[:count], refs[count:]
    even = lax.rem(lax.axis_index(axis), 2) == 0
    which = lane_iota() // plan.span
    me = lax.axis_index(axis_f)
    rows = pieces[0].shape[1]
    order = 0
    for piece in pieces:
        for part in range(piece.shape[1] // rows):
            start = (me ^ order) * rows
            order += 1
            for row in range(0, rows, SUB):
                at = part * rows + row
                to = pl.ds(pl.multiple_of(start + row, SUB), SUB)
                blocks = [1.0 / piece[f, at : at + SUB, :] for f in range(plan.freqs)]
                for f, block in enumerate(blocks):
                    natural[f, 0, to, :] = block
                first[0, to, :], second[0, to, :] = pack_edges(plan, even, which, blocks)


def taken(plan, lanes, v, f):
    column = ((lanes - plan.offsets[f]) & (LANES - 1)) + plan.halo
    return column, lax.rem(column, plan.ways) == v


def assemble_kernel(plan, axis_y, axis_x, src, got_a, got_b, tile, send_a, send_b):
    even_y = lax.rem(lax.axis_index(axis_y), 2) == 0
    even_x = lax.rem(lax.axis_index(axis_x), 2) == 0
    lanes = lane_iota()
    which = lanes // plan.span
    within = lanes - which * plan.span
    offset = jnp.zeros_like(lanes)
    for f in range(1, plan.freqs):
        offset = jnp.where(which == f, plan.offsets[f], offset)
    parts, rows = got_a.shape[0], got_a.shape[1]
    recipe = []
    for v in range(plan.ways):
        column = plan.ways * within + v
        inner = column - plan.halo
        beyond = inner - plan.tile
        outside = (inner < 0) | (beyond >= 0)
        main = (inner + offset) & (LANES - 1)
        side = which * plan.span + jnp.clip(jnp.where(inner < 0, column, beyond), 0, plan.halo - 1)
        recipe.append((outside, main, side))
    owner = [taken(plan, lanes, 0, f)[0] for f in range(plan.freqs)]
    owner = [lax.rem(column, plan.ways) for column in owner]
    whose = lax.rem(within, plan.ways)
    group = 4
    for part in range(parts):
        for chunk in range(0, rows, group * SUB):
            starts = range(chunk, min(chunk + group * SUB, rows), SUB)
            blocks, sides = [], []
            for row in starts:
                here = slice(row, row + SUB)
                blocks.append([turn(src[f, part, here, :], plan.offsets[f]) for f in range(plan.freqs)])
                a, b = got_a[part, here, :], got_b[part, here, :]
                sides.append((jnp.where(even_y, b, a), jnp.where(even_y, a, b)))
            for v in range(plan.ways):
                outside, main, side = recipe[v]
                mixed, edge = [], []
                for turned, (left, right) in zip(blocks, sides):
                    mix = turned[0]
                    for f in range(1, plan.freqs):
                        mix = jnp.where(owner[f] == v, turned[f], mix)
                    mixed.append(mix)
                    edge.append(jnp.where(whose == v, left, right))
                mixed = [pick(m, main) for m in mixed]
                edge = [pick(e, side) for e in edge]
                for row, m, e in zip(starts, mixed, edge):
                    tile[part, v, row : row + SUB, :] = jnp.where(outside, e, m)
    for part in range(parts):
        for v in range(plan.ways):
            for row in range(0, plan.halo, SUB):
                top = tile[part, v, row : row + SUB, :]
                start = rows - plan.halo + row
                low = tile[part, v, start : start + SUB, :]
                send_a[part, v, row : row + SUB, :] = jnp.where(even_x, low, top)
                send_b[part, v, row : row + SUB, :] = jnp.where(even_x, top, low)


def small_trig(theta):
    t = theta * theta
    sine = ((-1.9841270e-04 * t + 8.3333333e-03) * t - 1.6666667e-01) * t + 1.0
    cosine = ((-1.3888889e-03 * t + 4.1666667e-02) * t - 0.5) * t + 1.0
    return sine * theta, cosine


def migrate_kernel(plan, depth_list, order, axes, *refs):
    axis_f, axis_x, axis_y = axes
    first = depth_list[0] == 0
    last = depth_list[-1] == plan.depths - 1
    refs = list(refs)
    if first:
        core, core_a, core_b = refs[:3]
        vel, vel_a, vel_b = refs[3:6]
        refs = refs[6:]
    else:
        start, vel = refs[:2]
        refs = refs[2:]
    image, out = refs[:2]
    refs = refs[2:]
    if first:
        vel_out = None
        if not last:
            vel_out = refs[0]
            refs = refs[1:]
    hist = refs[0]
    halo, rows, ways, span = plan.halo, plan.rows, plan.ways, plan.span
    pad = SUB
    tiles = plan.tall // SUB
    gx, gy = lax.axis_index(axis_x), lax.axis_index(axis_y)
    even_x = lax.rem(gx, 2) == 0
    lanes = lane_iota()
    which = lanes // span
    within = lanes - which * span
    subl = lax.broadcasted_iota(jnp.int32, (SUB, LANES), 0)

    left_col, right_col = halo - 1, halo + plan.tile
    edge_left = (gy == 0) & (within == left_col // ways)
    edge_right = (gy == lax.axis_size(axis_y) - 1) & (within == right_col // ways)
    edge_top = (gx == 0) & (subl == (halo - 1) % SUB)
    edge_low = (gx == lax.axis_size(axis_x) - 1) & (subl == (halo + rows) % SUB)
    top_tile, low_tile = (halo - 1) // SUB, (halo + rows) // SUB

    def grid_edges(value, v, t):
        if v == left_col % ways:
            value = jnp.where(edge_left, 0.0, value)
        if v == right_col % ways:
            value = jnp.where(edge_right, 0.0, value)
        if t == top_tile:
            value = jnp.where(edge_top, 0.0, value)
        if t == low_tile:
            value = jnp.where(edge_low, 0.0, value)
        return value

    if first:
        for part in range(plan.parts):
            for v in range(ways):
                for row in range(0, halo, SUB):
                    a = core_a[part, v, row : row + SUB, :]
                    b = core_b[part, v, row : row + SUB, :]
                    hist[0, part, v, pad + row : pad + row + SUB, :] = jnp.where(even_x, b, a)
                    at = pad + halo + rows + row
                    hist[0, part, v, at : at + SUB, :] = jnp.where(even_x, a, b)
                for row in range(0, rows, SUB):
                    at = pad + halo + row
                    hist[0, part, v, at : at + SUB, :] = core[part, v, row : row + SUB, :]
    else:
        lead = SUB * depth_list[0]
        for part in range(plan.parts):
            for v in range(ways):
                for row in range(lead, plan.tall - lead, SUB):
                    hist[0, part, v, pad + row : pad + row + SUB, :] = start[
                        part, v, row - lead : row - lead + SUB, :
                    ]

    def slowness_at(v, t):
        row = t * SUB
        if not first:
            lead = SUB * (depth_list[0] + 1)
            return vel[v, row - lead : row - lead + SUB, :]
        if row < halo:
            a, b = vel_a[0, v, row : row + SUB, :], vel_b[0, v, row : row + SUB, :]
            return jnp.where(even_x, b, a)
        if row < halo + rows:
            return vel[0, v, row - halo : row - halo + SUB, :]
        row = row - halo - rows
        a, b = vel_a[0, v, row : row + SUB, :], vel_b[0, v, row : row + SUB, :]
        return jnp.where(even_x, a, b)

    weights = term_weights(order)
    count = plan.freqs
    total = count * lax.axis_size(axis_f)
    freq = (lax.axis_index(axis_f) * count + which).astype(jnp.float32)
    angular = (2.0 * math.pi) * (
        lowest_freq + (highest_freq - lowest_freq) * (freq + 0.5) / total
    )
    rate = angular * (depth_interval / (order + 1))

    def apply(seen, t, opening):
        old, now, new = seen
        for part in range(plan.parts):
            at = pad + t * SUB
            double, across = [], []
            for v in range(ways):
                mid = now[part, v, at : at + SUB, :]
                up = now[part, v, at - 1 : at - 1 + SUB, :]
                down = now[part, v, at + 1 : at + 1 + SUB, :]
                two = mid if opening else mid + mid
                double.append(two)
                across.append((mid + mid) + (up + down))
            wrap_low = pltpu.roll(across[-1], 1, 1)
            wrap_high = pltpu.roll(across[0], LANES - 1, 1)
            line = [wrap_low] + across + [wrap_high]
            pairs = [line[i] + line[i + 1] for i in range(ways + 1)]
            for v in range(ways):
                total_sum = pairs[v] + pairs[v + 1]
                if opening:
                    value = 0.125 * total_sum - double[v]
                else:
                    before = old[part, v, at : at + SUB, :]
                    value = (0.25 * total_sum - double[v]) - before
                new[part, v, at : at + SUB, :] = grid_edges(value, v, t)

    natural = lanes + halo
    source = natural // ways
    step_of = natural - source * ways

    def convert(t, slot, final):
        at, home = pad + t * SUB, t * SUB - halo
        if not final:
            tally = None
            for v in range(ways):
                fold = hist[0, 0, v, at : at + SUB, :]
                width = LANES // 2
                while width >= span:
                    fold = fold + pltpu.roll(fold, width, 1)
                    width //= 2
                fold = pick(fold, source)
                tally = fold if tally is None else jnp.where(step_of == v, fold, tally)
            image[slot, home : home + SUB, :] = tally
            return
        for part in range(plan.parts):
            spread_out = []
            for v in range(ways):
                index = jnp.zeros_like(lanes)
                for f in range(plan.freqs):
                    column, mine = taken(plan, lanes, v, f)
                    index = jnp.where(mine, f * span + column // ways, index)
                spread_out.append(pick(hist[0, part, v, at : at + SUB, :], index))
            tally = None
            for f in range(plan.freqs):
                value = spread_out[0]
                for v in range(1, ways):
                    value = jnp.where(taken(plan, lanes, v, f)[1], spread_out[v], value)
                value = turn(value, -plan.offsets[f])
                out[f, part, home : home + SUB, :] = value
                if part == 0:
                    tally = value if tally is None else tally + value
            if part == 0:
                image[slot, home : home + SUB, :] = tally

    for slot, depth in enumerate(depth_list):
        for t in range(depth, tiles - depth):
            apply((None, hist.at[0], hist.at[1]), t, True)

        def step(n, carry):
            view = hist.at[pl.ds(n - 2, 3)]
            seen = view.at[0], view.at[1], view.at[2]
            for t in range(depth, tiles - depth):
                apply(seen, t, False)
            return carry

        lax.fori_loop(2, order + 1, step, 0)
        final = depth == plan.depths - 1
        spread = depth * span + within
        inside = range(halo // SUB, (halo + rows) // SUB)
        waiting = []
        for t in range(depth + 1, tiles - depth - 1):
            at = pad + t * SUB
            trig = [small_trig(rate * pick(slowness_at(v, t), spread)) for v in range(ways)]
            twice = [cosine + cosine for _, cosine in trig]
            cells = [(part, v) for v in range(ways) for part in range(plan.parts)]
            near = [weights[order] * hist[order, p, v, at : at + SUB, :] for p, v in cells]
            far = [None] * len(cells)
            for n in range(order - 1, -1, -1):
                for i, (p, v) in enumerate(cells):
                    value = weights[n] * hist[n, p, v, at : at + SUB, :] + twice[v] * near[i]
                    if far[i] is not None:
                        value = value - far[i]
                    near[i], far[i] = value, near[i]
            for v in range(ways):
                sine, cosine = trig[v]
                real, imag = plan.parts * v, plan.parts * v + 1
                new_real = cosine * near[real] - sine * near[imag] - far[real]
                new_imag = sine * near[real] + cosine * near[imag] - far[imag]
                hist[0, 0, v, at : at + SUB, :] = new_real
                hist[0, 1, v, at : at + SUB, :] = new_imag
            if t in inside:
                waiting.append(t)
            if len(waiting) > 1:
                convert(waiting.pop(0), slot, final)
        for t in waiting:
            convert(t, slot, final)
    if not last:
        lead = SUB * (depth_list[-1] + 1)
        for part in range(plan.parts):
            for v in range(ways):
                for row in range(lead, plan.tall - lead, SUB):
                    at = pad + row
                    out[part, v, row - lead : row - lead + SUB, :] = hist[0, part, v, at : at + SUB, :]
    if first and not last:
        lead = SUB * (depth_list[-1] + 2)
        for v in range(ways):
            for row in range(lead, plan.tall - lead, SUB):
                vel_out[v, row - lead : row - lead + SUB, :] = slowness_at(v, row // SUB)


def swap(value, axis, odd):
    count = lax.axis_size(axis)
    pairs = []
    for i in range(odd, count - 1, 2):
        pairs += [(i, i + 1), (i + 1, i)]
    if not pairs:
        return jnp.zeros_like(value)
    return lax.ppermute(value, axis, pairs)


def gathered(value, axis):
    count = lax.axis_size(axis)
    assert count & (count - 1) == 0
    pieces, width = [value], 1
    while width < count:
        sent = pieces[0] if len(pieces) == 1 else jnp.concatenate(pieces, axis=1)
        pieces.append(lax.ppermute(sent, axis, [(i, i ^ width) for i in range(count)]))
        width *= 2
    return pieces


def sum_over(value, axis):
    count = lax.axis_size(axis)
    width = 1
    while width < count:
        value = value + lax.ppermute(value, axis, [(i, i ^ width) for i in range(count)])
        width *= 2
    return value


VMEM = pl.BlockSpec(memory_space=pltpu.VMEM)


def call(kernel, ins, outs, scratch=(), flops=0, name=None):
    moved = sum(4 * math.prod(x.shape) for x in ins) + sum(4 * math.prod(s) for s in outs)
    held = moved + sum(4 * math.prod(x.shape) for x in scratch)
    return pl.pallas_call(
        kernel,
        out_shape=[jax.ShapeDtypeStruct(s, jnp.float32) for s in outs],
        in_specs=[VMEM] * len(ins),
        out_specs=[VMEM] * len(outs),
        scratch_shapes=list(scratch),
        cost_estimate=pl.CostEstimate(flops=flops, bytes_accessed=moved, transcendentals=0),
        compiler_params=pltpu.CompilerParams(vmem_limit_bytes=held + (4 << 20)),
        name=name,
    )(*ins)


def assembled(plan, source, got_a, got_b):
    parts, rows = source.shape[1], source.shape[2]
    slab = (parts, plan.ways, plan.halo, LANES)
    return call(
        functools.partial(assemble_kernel, plan, "gy", "gx"),
        [source, got_a, got_b],
        [(parts, plan.ways, rows, LANES), slab, slab],
        name="assemble",
    )


def per_device(wavefield, velocity):
    order = ORDER
    plan = Plan(wavefield.shape, velocity.shape[0])
    axes = ("freq", "gx", "gy")
    freq_total = plan.freqs * lax.axis_size("freq")
    pieces = gathered(velocity, "freq")
    edge = (plan.parts, plan.rows, LANES)
    first, second = call(
        functools.partial(pack_kernel, plan, "gy"), [wavefield], [edge, edge], name="pack"
    )
    wave_a, wave_b = swap(first, "gy", 0), swap(second, "gy", 1)
    edge = (1, plan.rows, LANES)
    slowness, first, second = call(
        functools.partial(pack_slowness_kernel, plan, "gy", "freq", len(pieces)),
        pieces,
        [(plan.depths, 1, plan.rows, plan.tile), edge, edge],
        name="pack_slowness",
    )
    wave_a, wave_b, first, second = lax.optimization_barrier((wave_a, wave_b, first, second))
    slow_a, slow_b = swap(first, "gy", 0), swap(second, "gy", 1)
    tile, send_a, send_b = assembled(plan, wavefield, wave_a, wave_b)
    wave = tile, swap(send_a, "gx", 0), swap(send_b, "gx", 1)
    tile, send_a, send_b = assembled(plan, slowness, slow_a, slow_b)
    slabs = tile, swap(send_a, "gx", 0), swap(send_b, "gx", 1)
    depths = list(range(plan.depths))
    head, tail = depths[:-1], depths[-1:]
    kept = plan.tall - 2 * SUB * len(head)
    need = plan.tall - 2 * SUB * (len(head) + 1)
    hist = pltpu.VMEM((order + 1, plan.parts, plan.ways, plan.tall + 2 * SUB, LANES), jnp.float32)
    square = (plan.rows, plan.tile)
    image_head, middle, speed_mid = call(
        functools.partial(migrate_kernel, plan, head, order, axes),
        [*wave, *slabs],
        [(len(head),) + square, (plan.parts, plan.ways, kept, LANES), (plan.ways, need, LANES)],
        [hist],
        flops=30_000_000,
        name="head",
    )
    image_tail, last = call(
        functools.partial(migrate_kernel, plan, tail, order, axes),
        [middle, speed_mid],
        [(len(tail),) + square, wavefield.shape],
        [hist],
        flops=30_000_000,
        name="tail",
    )
    scale = 1.0 / math.sqrt(freq_total)
    image = jnp.concatenate([sum_over(image_head, "freq"), sum_over(image_tail, "freq")]) * scale
    return image, last


def solution(mesh):
    placed = (P("freq", None, "gx", "gy"), P(None, ("gx", "freq"), "gy"))
    return jax.shard_map(
        per_device,
        mesh=mesh,
        in_specs=placed,
        out_specs=(P(None, "gx", "gy"), P("freq", None, "gx", "gy")),
        check_vma=False,
    )
```

time: 180 us -> 59.9 us (0.33)
  Pallas kernels: 145 us -> 27.6 us
    pallas_call x6, Pallas kernels: 145 us -> 27.6 us  [call(): pl.pallas_call(kernel, out_shape=[jax.ShapeDtypeStruct(s, jnp.float32) fo...]
  transfers between devices with their start and end apart: 11 -> 11, of which waited for: 6 -> 6; matrix products, arithmetic and copies ran while one was open for 1% -> 0% of each run, Pallas kernels for 24% -> 11%
where the time goes in v2:
time: 59.9 us; the launch traced here: 59.7 us
  Pallas kernels  27.6 us (46%)
  waiting for transfers between devices  14.7 us (25%)
  starting transfers between devices  13.9 us (23%)
  local copies, waits for them, and re-layouts  1.94 us (3%)
  between operations  0.77 us (1%)
  other arithmetic  0.76 us (1%)
    pallas_call x6, Pallas kernels, call(): pl.pallas_call(kernel, out_shape=[jax.ShapeDtypeStruct(s, jnp.float32) fo...  27.6 us
    ppermute x8, waiting for transfers between devices, swap(): return lax.ppermute(value, axis, pairs)  11.9 us
    ppermute x8, starting transfers between devices, swap(): return lax.ppermute(value, axis, pairs)  10.3 us
    ppermute x2, waiting for transfers between devices, sum_over(): lax.ppermute(value, axis, [(i, i ^ width) for i in range(count)])  2.78 us
    ppermute x2, starting transfers between devices, sum_over(): lax.ppermute(value, axis, [(i, i ^ width) for i in range(count)])  2.09 us
    unnamed x6, local copies, waits for them, and re-layouts  1.94 us
    ppermute x1, starting transfers between devices, gathered(): lax.ppermute(sent, axis, [(i, i ^ width) for i in range(count)])  1.56 us
  transfers between devices with their start and end apart: 11, of which 6 were waited for; matrix products, arithmetic and copies ran while one was open for 0% of the time, Pallas kernels for 11%

profile of v2, /device:TPU:20, one launch (start us, length us, event | category | flops | bytes accessed | tf_op | source)
XLA Modules:
  0.0 59.7 jit_solution(5841986424065275001)
XLA Ops:
  0.6 1.6 %collective-permute-start.2 = (f32[4,64,128]{2,1,0:T(8,128)}, f32[4,64,128]{2,1,0:T(8,128)S(1)}, u32[]{:S(2)}, u32[]{:S(2)}) collective-permute-start(f32[4,64,128]{2,1,0:T(8,128)} %refs_0_.1), channel_id=1, source_target_pairs={{0,16},{16,0},{1,17},{17,1},{2,18},{18,2},{3,19},{19,3},{4,20},{20... | collective-permute-start | bytes 393224 | tf_op jit(solution)/shard_map/ppermute | solution.py:405
  2.2 0.0 copy-start
  2.2 1.0 %copy-done = f32[4,2,128,128]{3,2,1,0:T(8,128)S(1)} copy-done((f32[4,2,128,128]{3,2,1,0:T(8,128)S(1)}, f32[4,2,128,128]{3,2,1,0:T(8,128)}, u32[]{:S(2)}) %copy-start) | copy-done | bytes 524312
  3.2 0.0 copy-start.1
  3.2 0.3 pack.1
  3.5 1.6 %collective-permute-start = (f32[2,128,128]{2,1,0:T(8,128)S(1)}, f32[2,128,128]{2,1,0:T(8,128)S(1)}, u32[]{:S(2)}, u32[]{:S(2)}) collective-permute-start(f32[2,128,128]{2,1,0:T(8,128)S(1)} %get-tuple-element.22), channel_id=1, source_target_pairs={{0,1},{1,0},{2,3},{3,2},{4,5},{5,4},{6,7},{7,6},{8,9},{9,8},{10,11... | collective-permute-start | bytes 393224 | tf_op jit(solution)/shard_map/ppermute | solution.py:396
  5.1 1.9 %collective-permute-start.1 = (f32[2,128,128]{2,1,0:T(8,128)S(1)}, f32[2,128,128]{2,1,0:T(8,128)S(1)}, u32[]{:S(2)}, u32[]{:S(2)}) collective-permute-start(f32[2,128,128]{2,1,0:T(8,128)S(1)} %get-tuple-element.23), channel_id=1, source_target_pairs={{1,2},{2,1},{5,6},{6,5},{9,10},{10,9},{13,14},{14,13},{17,18},{18,... | collective-permute-start | bytes 393224 | tf_op jit(solution)/shard_map/ppermute | solution.py:396
  7.1 0.0 collective-permute-done.2.refs_1_
  7.1 0.0 copy-start.2
  7.1 0.9 %copy-done.2 = f32[4,64,128]{2,1,0:T(8,128)S(1)} copy-done((f32[4,64,128]{2,1,0:T(8,128)S(1)}, f32[4,64,128]{2,1,0:T(8,128)}, u32[]{:S(2)}) %copy-start.2) | copy-done | bytes 131096
  8.0 0.2 pack_slowness.1
  8.2 0.4 collective-permute-done.got_a
  8.5 3.5 %collective-permute-done.1.got_b = f32[2,128,128]{2,1,0:T(8,128)S(1)} collective-permute-done((f32[2,128,128]{2,1,0:T(8,128)S(1)}, f32[2,128,128]{2,1,0:T(8,128)S(1)}, u32[]{:S(2)}, u32[]{:S(2)}) %collective-permute-start.1) | collective-permute-done | bytes 131104 | tf_op jit(solution)/shard_map/ppermute | solution.py:396
  12.0 0.0 copy-done.1
  12.0 1.5 %assemble.2 = (f32[2,6,128,128]{3,2,1,0:T(8,128)S(1)}, f32[2,6,32,128]{3,2,1,0:T(8,128)S(1)}, f32[2,6,32,128]{3,2,1,0:T(8,128)S(1)}) custom-call(f32[4,2,128,128]{3,2,1,0:T(8,128)S(1)} %copy-done.1, f32[2,128,128]{2,1,0:T(8,128)S(1)} %collective-permute-done.got_a, f32[2,128,128]{2,1,0:T(8,128)S(1)} %collective-permute-done.1.got_b), custom_call_target="tpu_custom_call" | custom-call | bytes 1966080 | tf_op jit(solution)/shard_map/assemble/pallas_call | solution.py:425
  13.5 0.1 collective-permute-start.3
  13.6 2.5 %collective-permute-start.4 = (f32[2,6,32,128]{3,2,1,0:T(8,128)S(1)}, f32[2,6,32,128]{3,2,1,0:T(8,128)S(1)}, u32[]{:S(2)}, u32[]{:S(2)}) collective-permute-start(f32[2,6,32,128]{3,2,1,0:T(8,128)S(1)} %get-tuple-element.30), channel_id=1, source_target_pairs={{4,8},{8,4},{5,9},{9,5},{6,10},{10,6},{7,11},{11,7},{20,24},{24,20... | collective-permute-start | bytes 589832 | tf_op jit(solution)/shard_map/ppermute | solution.py:396
  16.1 0.1 collective-permute-start.5
  16.2 1.9 %collective-permute-start.6 = (f32[1,128,128]{2,1,0:T(8,128)S(1)}, f32[1,128,128]{2,1,0:T(8,128)S(1)}, u32[]{:S(2)}, u32[]{:S(2)}) collective-permute-start(f32[1,128,128]{2,1,0:T(8,128)S(1)} %get-tuple-element.33), channel_id=1, source_target_pairs={{1,2},{2,1},{5,6},{6,5},{9,10},{10,9},{13,14},{14,13},{17,18},{18,... | collective-permute-start | bytes 196616 | tf_op jit(solution)/shard_map/ppermute | solution.py:396
  18.1 2.3 %collective-permute-done.5.got_a = f32[1,128,128]{2,1,0:T(8,128)S(1)} collective-permute-done((f32[1,128,128]{2,1,0:T(8,128)S(1)}, f32[1,128,128]{2,1,0:T(8,128)S(1)}, u32[]{:S(2)}, u32[]{:S(2)}) %collective-permute-start.5) | collective-permute-done | bytes 65568 | tf_op jit(solution)/shard_map/ppermute | solution.py:396
  20.4 1.9 %collective-permute-done.6.got_b = f32[1,128,128]{2,1,0:T(8,128)S(1)} collective-permute-done((f32[1,128,128]{2,1,0:T(8,128)S(1)}, f32[1,128,128]{2,1,0:T(8,128)S(1)}, u32[]{:S(2)}, u32[]{:S(2)}) %collective-permute-start.6) | collective-permute-done | bytes 65568 | tf_op jit(solution)/shard_map/ppermute | solution.py:396
  22.4 0.7 %assemble.3 = (f32[1,6,128,128]{3,2,1,0:T(8,128)S(1)}, f32[1,6,32,128]{3,2,1,0:T(8,128)S(1)}, f32[1,6,32,128]{3,2,1,0:T(8,128)S(1)}) custom-call(f32[4,1,128,128]{3,2,1,0:T(8,128)S(1)} %get-tuple-element.31.src, f32[1,128,128]{2,1,0:T(8,128)S(1)} %collective-permute-done.5.got_a, f32[1,128,128]{2,1,0:T(8,128)S(1)} %collective-permute-done.6.got_b), custom_call_target="tpu_custom_call" | custom-call | bytes 983040 | tf_op jit(solution)/shard_map/assemble/pallas_call | solution.py:425
  23.1 0.1 collective-permute-start.7
  23.2 2.1 %collective-permute-start.8 = (f32[1,6,32,128]{3,2,1,0:T(8,128)S(1)}, f32[1,6,32,128]{3,2,1,0:T(8,128)S(1)}, u32[]{:S(2)}, u32[]{:S(2)}) collective-permute-start(f32[1,6,32,128]{3,2,1,0:T(8,128)S(1)} %get-tuple-element.36), channel_id=1, source_target_pairs={{4,8},{8,4},{5,9},{9,5},{6,10},{10,6},{7,11},{11,7},{20,24},{24,20... | collective-permute-start | bytes 294920 | tf_op jit(solution)/shard_map/ppermute | solution.py:396
  25.3 0.0 collective-permute-done.7.refs_4_
  25.3 3.8 %collective-permute-done.8.refs_5_ = f32[1,6,32,128]{3,2,1,0:T(8,128)S(1)} collective-permute-done((f32[1,6,32,128]{3,2,1,0:T(8,128)S(1)}, f32[1,6,32,128]{3,2,1,0:T(8,128)S(1)}, u32[]{:S(2)}, u32[]{:S(2)}) %collective-permute-start.8) | collective-permute-done | bytes 98336 | tf_op jit(solution)/shard_map/ppermute | solution.py:396
  29.1 0.0 collective-permute-done.3.refs_1_
  29.1 0.0 collective-permute-done.4.refs_2_
  29.1 19.3 %head.1 = (f32[3,128,128]{2,1,0:T(8,128)S(1)}, f32[2,6,144,128]{3,2,1,0:T(8,128)S(1)}, f32[6,128,128]{2,1,0:T(8,128)S(1)}) custom-call(f32[2,6,128,128]{3,2,1,0:T(8,128)S(1)} %get-tuple-element.28.refs_0_, f32[2,6,32,128]{3,2,1,0:T(8,128)S(1)} %collective-permute-done.3.refs_1_, f32[2,6,32,128]{3,2,1,0:T(8,128)S(1)} %collective-permute-done.4.refs_2_, ...), custom_call_target="tpu_custom_call" | custom-call | flops 30000000 | bytes 3244032 | tf_op jit(solution)/shard_map/head/pallas_call | solution.py:425
  48.4 0.6 %collective-permute-start.9 = (f32[3,128,128]{2,1,0:T(8,128)S(1)}, f32[3,128,128]{2,1,0:T(8,128)S(1)}, u32[]{:S(2)}, u32[]{:S(2)}) collective-permute-start(f32[3,128,128]{2,1,0:T(8,128)S(1)} %get-tuple-element.37), channel_id=1, source_target_pairs={{0,16},{16,0},{1,17},{17,1},{2,18},{18,2},{3,19},{19,3},{4,20},{20... | collective-permute-start | bytes 589832 | tf_op jit(solution)/shard_map/ppermute | solution.py:414
  49.0 5.6 %tail.1 = (f32[1,128,128]{2,1,0:T(8,128)S(1)}, f32[4,2,128,128]{3,2,1,0:T(8,128)}) custom-call(f32[2,6,144,128]{3,2,1,0:T(8,128)S(1)} %get-tuple-element.38.refs_0_, f32[6,128,128]{2,1,0:T(8,128)S(1)} %get-tuple-element.39.refs_1_), custom_call_target="tpu_custom_call" | custom-call | flops 30000000 | bytes 1867776 | tf_op jit(solution)/shard_map/tail/pallas_call | solution.py:425
  54.6 1.5 %collective-permute-start.10 = (f32[1,128,128]{2,1,0:T(8,128)S(1)}, f32[1,128,128]{2,1,0:T(8,128)S(1)}, u32[]{:S(2)}, u32[]{:S(2)}) collective-permute-start(f32[1,128,128]{2,1,0:T(8,128)S(1)} %get-tuple-element.40), channel_id=1, source_target_pairs={{0,16},{16,0},{1,17},{17,1},{2,18},{18,2},{3,19},{19,3},{4,20},{20... | collective-permute-start | bytes 196616 | tf_op jit(solution)/shard_map/ppermute | solution.py:414
  56.1 2.8 %collective-permute-done.10 = f32[1,128,128]{2,1,0:T(8,128)S(1)} collective-permute-done((f32[1,128,128]{2,1,0:T(8,128)S(1)}, f32[1,128,128]{2,1,0:T(8,128)S(1)}, u32[]{:S(2)}, u32[]{:S(2)}) %collective-permute-start.10) | collective-permute-done | bytes 65568 | tf_op jit(solution)/shard_map/ppermute | solution.py:414
  58.9 0.0 collective-permute-done.9
  59.0 0.7 %maximum_multiply_fusion = f32[4,128,128]{2,1,0:T(8,128)} fusion(f32[1,128,128]{2,1,0:T(8,128)S(1)} %add.7, f32[3,128,128]{2,1,0:T(8,128)S(1)} %add.6), kind=kLoop, calls=%fused_computation | loop fusion | flops 131072 | bytes 524288 | tf_op jit(solution)/shard_map/mul | solution.py:495
  (2 shorter events, 0.0 us)
Async XLA Ops:
  0.6 6.4 %collective-permute-start.2 = (f32[4,64,128]{2,1,0:T(8,128)}, f32[4,64,128]{2,1,0:T(8,128)S(1)}, u32[]{:S(2)}, u32[]{:S(2)}) collective-permute-start(f32[4,64,128]{2,1,0:T(8,128)} %refs_0_.1), channel_id=1, source_target_pairs={{0,16},{16,0},{1,17},{17,1},{2,18},{18,2},{3,19},{19,3},{4,20},{20... | collective-permute-start | bytes 393224 | tf_op jit(solution)/shard_map/ppermute | solution.py:405
  2.2 1.0 %copy-start = (f32[4,2,128,128]{3,2,1,0:T(8,128)S(1)}, f32[4,2,128,128]{3,2,1,0:T(8,128)}, u32[]{:S(2)}) copy-start(f32[4,2,128,128]{3,2,1,0:T(8,128)} %src.3) | copy-start | bytes 1572868
  3.2 8.8 %copy-start.1 = (f32[4,2,128,128]{3,2,1,0:T(8,128)S(1)}, f32[4,2,128,128]{3,2,1,0:T(8,128)}, u32[]{:S(2)}) copy-start(f32[4,2,128,128]{3,2,1,0:T(8,128)} %src.3) | copy-start | bytes 1572868
  3.5 5.0 %collective-permute-start = (f32[2,128,128]{2,1,0:T(8,128)S(1)}, f32[2,128,128]{2,1,0:T(8,128)S(1)}, u32[]{:S(2)}, u32[]{:S(2)}) collective-permute-start(f32[2,128,128]{2,1,0:T(8,128)S(1)} %get-tuple-element.22), channel_id=1, source_target_pairs={{0,1},{1,0},{2,3},{3,2},{4,5},{5,4},{6,7},{7,6},{8,9},{9,8},{10,11... | collective-permute-start | bytes 393224 | tf_op jit(solution)/shard_map/ppermute | solution.py:396
  5.1 6.8 %collective-permute-start.1 = (f32[2,128,128]{2,1,0:T(8,128)S(1)}, f32[2,128,128]{2,1,0:T(8,128)S(1)}, u32[]{:S(2)}, u32[]{:S(2)}) collective-permute-start(f32[2,128,128]{2,1,0:T(8,128)S(1)} %get-tuple-element.23), channel_id=1, source_target_pairs={{1,2},{2,1},{5,6},{6,5},{9,10},{10,9},{13,14},{14,13},{17,18},{18,... | collective-permute-start | bytes 393224 | tf_op jit(solution)/shard_map/ppermute | solution.py:396
  7.1 0.9 %copy-start.2 = (f32[4,64,128]{2,1,0:T(8,128)S(1)}, f32[4,64,128]{2,1,0:T(8,128)}, u32[]{:S(2)}) copy-start(f32[4,64,128]{2,1,0:T(8,128)} %refs_0_.1) | copy-start | bytes 393220
  13.5 15.6 %collective-permute-start.3 = (f32[2,6,32,128]{3,2,1,0:T(8,128)S(1)}, f32[2,6,32,128]{3,2,1,0:T(8,128)S(1)}, u32[]{:S(2)}, u32[]{:S(2)}) collective-permute-start(f32[2,6,32,128]{3,2,1,0:T(8,128)S(1)} %get-tuple-element.29), channel_id=1, source_target_pairs={{0,4},{4,0},{8,12},{12,8},{1,5},{5,1},{9,13},{13,9},{2,6},{6,2},{1... | collective-permute-start | bytes 589832 | tf_op jit(solution)/shard_map/ppermute | solution.py:396
  13.6 15.5 %collective-permute-start.4 = (f32[2,6,32,128]{3,2,1,0:T(8,128)S(1)}, f32[2,6,32,128]{3,2,1,0:T(8,128)S(1)}, u32[]{:S(2)}, u32[]{:S(2)}) collective-permute-start(f32[2,6,32,128]{3,2,1,0:T(8,128)S(1)} %get-tuple-element.30), channel_id=1, source_target_pairs={{4,8},{8,4},{5,9},{9,5},{6,10},{10,6},{7,11},{11,7},{20,24},{24,20... | collective-permute-start | bytes 589832 | tf_op jit(solution)/shard_map/ppermute | solution.py:396
  16.1 4.3 %collective-permute-start.5 = (f32[1,128,128]{2,1,0:T(8,128)S(1)}, f32[1,128,128]{2,1,0:T(8,128)S(1)}, u32[]{:S(2)}, u32[]{:S(2)}) collective-permute-start(f32[1,128,128]{2,1,0:T(8,128)S(1)} %get-tuple-element.32), channel_id=1, source_target_pairs={{0,1},{1,0},{2,3},{3,2},{4,5},{5,4},{6,7},{7,6},{8,9},{9,8},{10,11... | collective-permute-start | bytes 196616 | tf_op jit(solution)/shard_map/ppermute | solution.py:396
  16.2 6.2 %collective-permute-start.6 = (f32[1,128,128]{2,1,0:T(8,128)S(1)}, f32[1,128,128]{2,1,0:T(8,128)S(1)}, u32[]{:S(2)}, u32[]{:S(2)}) collective-permute-start(f32[1,128,128]{2,1,0:T(8,128)S(1)} %get-tuple-element.33), channel_id=1, source_target_pairs={{1,2},{2,1},{5,6},{6,5},{9,10},{10,9},{13,14},{14,13},{17,18},{18,... | collective-permute-start | bytes 196616 | tf_op jit(solution)/shard_map/ppermute | solution.py:396
  23.1 2.2 %collective-permute-start.7 = (f32[1,6,32,128]{3,2,1,0:T(8,128)S(1)}, f32[1,6,32,128]{3,2,1,0:T(8,128)S(1)}, u32[]{:S(2)}, u32[]{:S(2)}) collective-permute-start(f32[1,6,32,128]{3,2,1,0:T(8,128)S(1)} %get-tuple-element.35), channel_id=1, source_target_pairs={{0,4},{4,0},{8,12},{12,8},{1,5},{5,1},{9,13},{13,9},{2,6},{6,2},{1... | collective-permute-start | bytes 294920 | tf_op jit(solution)/shard_map/ppermute | solution.py:396
  23.2 5.9 %collective-permute-start.8 = (f32[1,6,32,128]{3,2,1,0:T(8,128)S(1)}, f32[1,6,32,128]{3,2,1,0:T(8,128)S(1)}, u32[]{:S(2)}, u32[]{:S(2)}) collective-permute-start(f32[1,6,32,128]{3,2,1,0:T(8,128)S(1)} %get-tuple-element.36), channel_id=1, source_target_pairs={{4,8},{8,4},{5,9},{9,5},{6,10},{10,6},{7,11},{11,7},{20,24},{24,20... | collective-permute-start | bytes 294920 | tf_op jit(solution)/shard_map/ppermute | solution.py:396
  48.4 10.5 %collective-permute-start.9 = (f32[3,128,128]{2,1,0:T(8,128)S(1)}, f32[3,128,128]{2,1,0:T(8,128)S(1)}, u32[]{:S(2)}, u32[]{:S(2)}) collective-permute-start(f32[3,128,128]{2,1,0:T(8,128)S(1)} %get-tuple-element.37), channel_id=1, source_target_pairs={{0,16},{16,0},{1,17},{17,1},{2,18},{18,2},{3,19},{19,3},{4,20},{20... | collective-permute-start | bytes 589832 | tf_op jit(solution)/shard_map/ppermute | solution.py:414
  54.6 4.3 %collective-permute-start.10 = (f32[1,128,128]{2,1,0:T(8,128)S(1)}, f32[1,128,128]{2,1,0:T(8,128)S(1)}, u32[]{:S(2)}, u32[]{:S(2)}) collective-permute-start(f32[1,128,128]{2,1,0:T(8,128)S(1)} %get-tuple-element.40), channel_id=1, source_target_pairs={{0,16},{16,0},{1,17},{17,1},{2,18},{18,2},{3,19},{19,3},{4,20},{20... | collective-permute-start | bytes 196616 | tf_op jit(solution)/shard_map/ppermute | solution.py:414

commit v3 on v2

--- a/solution.py
+++ b/solution.py
@@ -77,19 +77,24 @@
     return jnp.where(even, high, low), jnp.where(even, low, high)
 
 
-def pack_kernel(plan, axis, src, first, second):
+def pack_kernel(plan, axis, src, speed, first, second, held, slow):
     even = lax.rem(lax.axis_index(axis), 2) == 0
     which = lane_iota() // plan.span
-    parts, rows = first.shape[0], first.shape[1]
-    for part in range(parts):
-        for row in range(0, rows, SUB):
+    for row in range(0, speed.shape[1], SUB):
+        for f in range(plan.freqs):
+            slow[f, row : row + SUB, :] = 1.0 / speed[f, row : row + SUB, :]
+    for part in range(plan.parts):
+        for row in range(0, plan.rows, SUB):
             here = slice(row, row + SUB)
             blocks = [src[f, part, here, :] for f in range(plan.freqs)]
+            for f, block in enumerate(blocks):
+                held[f, part, here, :] = block
             first[part, here, :], second[part, here, :] = pack_edges(plan, even, which, blocks)
 
 
 def pack_slowness_kernel(plan, axis, axis_f, count, *refs):
-    pieces, (natural, first, second) = refs[:count], refs[count:]
+    first2, second2 = refs[:2]
+    pieces, (natural, first, second) = refs[2 : 2 + count], refs[2 + count :]
     even = lax.rem(lax.axis_index(axis), 2) == 0
     which = lane_iota() // plan.span
     me = lax.axis_index(axis_f)
@@ -98,14 +103,22 @@
     for piece in pieces:
         for part in range(piece.shape[1] // rows):
             start = (me ^ order) * rows
-            order += 1
             for row in range(0, rows, SUB):
                 at = part * rows + row
                 to = pl.ds(pl.multiple_of(start + row, SUB), SUB)
-                blocks = [1.0 / piece[f, at : at + SUB, :] for f in range(plan.freqs)]
+                blocks = [piece[f, at : at + SUB, :] for f in range(plan.freqs)]
+                if order > 0:
+                    blocks = [1.0 / block for block in blocks]
                 for f, block in enumerate(blocks):
-                    natural[f, 0, to, :] = block
-                first[0, to, :], second[0, to, :] = pack_edges(plan, even, which, blocks)
+                    natural[f, to, :] = block
+                edges = pack_edges(plan, even, which, blocks)
+                first[plan.parts, to, :], second[plan.parts, to, :] = edges
+            order += 1
+    for part in range(plan.parts):
+        for row in range(0, plan.rows, SUB):
+            here = slice(row, row + SUB)
+            first[part, here, :] = first2[part, here, :]
+            second[part, here, :] = second2[part, here, :]
 
 
 def taken(plan, lanes, v, f):
@@ -113,7 +126,7 @@
     return column, lax.rem(column, plan.ways) == v
 
 
-def assemble_kernel(plan, axis_y, axis_x, src, got_a, got_b, tile, send_a, send_b):
+def assemble_kernel(plan, axis_y, axis_x, src, slow, got_a, got_b, tile, send_a, send_b):
     even_y = lax.rem(lax.axis_index(axis_y), 2) == 0
     even_x = lax.rem(lax.axis_index(axis_x), 2) == 0
     lanes = lane_iota()
@@ -142,7 +155,11 @@
             blocks, sides = [], []
             for row in starts:
                 here = slice(row, row + SUB)
-                blocks.append([turn(src[f, part, here, :], plan.offsets[f]) for f in range(plan.freqs)])
+                found = [
+                    src[f, part, here, :] if part < plan.parts else slow[f, here, :]
+                    for f in range(plan.freqs)
+                ]
+                blocks.append([turn(block, plan.offsets[f]) for f, block in enumerate(found)])
                 a, b = got_a[part, here, :], got_b[part, here, :]
                 sides.append((jnp.where(even_y, b, a), jnp.where(even_y, a, b)))
             for v in range(plan.ways):
@@ -175,53 +192,113 @@
     return sine * theta, cosine
 
 
+class Tile:
+
+    def __init__(self, plan, axes):
+        self.plan = plan
+        _, axis_x, axis_y = axes
+        gx, gy = lax.axis_index(axis_x), lax.axis_index(axis_y)
+        self.even_x = lax.rem(gx, 2) == 0
+        self.lanes = lane_iota()
+        self.which = self.lanes // plan.span
+        self.within = self.lanes - self.which * plan.span
+        subl = lax.broadcasted_iota(jnp.int32, (SUB, LANES), 0)
+        self.left_col, self.right_col = plan.halo - 1, plan.halo + plan.tile
+        top, low = plan.halo - 1, plan.halo + plan.rows
+        ways = plan.ways
+        self.edge_left = (gy == 0) & (self.within == self.left_col // ways)
+        self.edge_right = (gy == lax.axis_size(axis_y) - 1) & (self.within == self.right_col // ways)
+        self.edge_top = (gx == 0) & (subl == top % SUB)
+        self.edge_low = (gx == lax.axis_size(axis_x) - 1) & (subl == low % SUB)
+        self.top_tile, self.low_tile = top // SUB, low // SUB
+
+    def grid_edges(self, value, v, t):
+        ways = self.plan.ways
+        if v == self.left_col % ways:
+            value = jnp.where(self.edge_left, 0.0, value)
+        if v == self.right_col % ways:
+            value = jnp.where(self.edge_right, 0.0, value)
+        if t == self.top_tile:
+            value = jnp.where(self.edge_top, 0.0, value)
+        if t == self.low_tile:
+            value = jnp.where(self.edge_low, 0.0, value)
+        return value
+
+    def apply(self, old, now, new, t, at):
+        ways = self.plan.ways
+        for part in range(self.plan.parts):
+            double, across = [], []
+            for v in range(ways):
+                mid = now[part, v, at : at + SUB, :]
+                up = now[part, v, at - 1 : at - 1 + SUB, :]
+                down = now[part, v, at + 1 : at + 1 + SUB, :]
+                two = mid + mid
+                double.append(mid if old is None else two)
+                across.append(two + (up + down))
+            wrap_low = pltpu.roll(across[-1], 1, 1)
+            wrap_high = pltpu.roll(across[0], LANES - 1, 1)
+            line = [wrap_low] + across + [wrap_high]
+            pairs = [line[i] + line[i + 1] for i in range(ways + 1)]
+            for v in range(ways):
+                whole = pairs[v] + pairs[v + 1]
+                if old is None:
+                    value = 0.125 * whole - double[v]
+                else:
+                    value = (0.25 * whole - double[v]) - old[part, v, at : at + SUB, :]
+                new[part, v, at : at + SUB, :] = self.grid_edges(value, v, t)
+
+    def terms(self, hist, order, rows):
+        for t, at in rows:
+            self.apply(None, hist.at[0], hist.at[1], t, at)
+
+        def step(n, carry):
+            view = hist.at[pl.ds(n - 2, 3)]
+            for t, at in rows:
+                self.apply(view.at[0], view.at[1], view.at[2], t, at)
+            return carry
+
+        lax.fori_loop(2, order + 1, step, 0)
+
+
+def inner_tiles(plan):
+    return range((plan.halo + SUB) // SUB, (plan.halo + plan.rows - SUB) // SUB)
+
+
+def inner_kernel(plan, order, axes, tile, hist):
+    state = Tile(plan, axes)
+    for part in range(plan.parts):
+        for v in range(plan.ways):
+            for row in range(0, plan.rows, SUB):
+                hist[0, part, v, SUB + row : SUB + row + SUB, :] = tile[part, v, row : row + SUB, :]
+    first = plan.halo // SUB
+    rows = [(first + i, SUB + i * SUB) for i in range(plan.rows // SUB)]
+    state.terms(hist, order, rows)
+
+
 def migrate_kernel(plan, depth_list, order, axes, *refs):
-    axis_f, axis_x, axis_y = axes
+    axis_f = axes[0]
     first = depth_list[0] == 0
     last = depth_list[-1] == plan.depths - 1
     refs = list(refs)
     if first:
-        core, core_a, core_b = refs[:3]
-        vel, vel_a, vel_b = refs[3:6]
-        refs = refs[6:]
+        core, core_a, core_b, known = refs[:4]
+        refs = refs[4:]
     else:
         start, vel = refs[:2]
         refs = refs[2:]
     image, out = refs[:2]
     refs = refs[2:]
-    if first:
-        vel_out = None
-        if not last:
-            vel_out = refs[0]
-            refs = refs[1:]
+    if first and not last:
+        vel_out = refs[0]
+        refs = refs[1:]
     hist = refs[0]
     halo, rows, ways, span = plan.halo, plan.rows, plan.ways, plan.span
     pad = SUB
     tiles = plan.tall // SUB
-    gx, gy = lax.axis_index(axis_x), lax.axis_index(axis_y)
-    even_x = lax.rem(gx, 2) == 0
-    lanes = lane_iota()
-    which = lanes // span
-    within = lanes - which * span
-    subl = lax.broadcasted_iota(jnp.int32, (SUB, LANES), 0)
-
-    left_col, right_col = halo - 1, halo + plan.tile
-    edge_left = (gy == 0) & (within == left_col // ways)
-    edge_right = (gy == lax.axis_size(axis_y) - 1) & (within == right_col // ways)
-    edge_top = (gx == 0) & (subl == (halo - 1) % SUB)
-    edge_low = (gx == lax.axis_size(axis_x) - 1) & (subl == (halo + rows) % SUB)
-    top_tile, low_tile = (halo - 1) // SUB, (halo + rows) // SUB
-
-    def grid_edges(value, v, t):
-        if v == left_col % ways:
-            value = jnp.where(edge_left, 0.0, value)
-        if v == right_col % ways:
-            value = jnp.where(edge_right, 0.0, value)
-        if t == top_tile:
-            value = jnp.where(edge_top, 0.0, value)
-        if t == low_tile:
-            value = jnp.where(edge_low, 0.0, value)
-        return value
+    state = Tile(plan, axes)
+    even_x, lanes, which, within = state.even_x, state.lanes, state.which, state.within
+    inner = inner_tiles(plan)
+    skip = halo
 
     if first:
         for part in range(plan.parts):
@@ -232,9 +309,17 @@
                     hist[0, part, v, pad + row : pad + row + SUB, :] = jnp.where(even_x, b, a)
                     at = pad + halo + rows + row
                     hist[0, part, v, at : at + SUB, :] = jnp.where(even_x, a, b)
-                for row in range(0, rows, SUB):
-                    at = pad + halo + row
+                for t in range(halo // SUB, (halo + rows) // SUB):
+                    if t in inner[1:-1]:
+                        continue
+                    at, row = pad + t * SUB, t * SUB - halo
                     hist[0, part, v, at : at + SUB, :] = core[part, v, row : row + SUB, :]
+                for t in (inner[0], inner[-1]):
+                    at = pad + t * SUB
+                    for n in range(1, order):
+                        hist[n, part, v, at : at + SUB, :] = known[
+                            n, part, v, at - skip : at - skip + SUB, :
+                        ]
     else:
         lead = SUB * depth_list[0]
         for part in range(plan.parts):
@@ -249,13 +334,14 @@
         if not first:
             lead = SUB * (depth_list[0] + 1)
             return vel[v, row - lead : row - lead + SUB, :]
+        part = plan.parts
         if row < halo:
-            a, b = vel_a[0, v, row : row + SUB, :], vel_b[0, v, row : row + SUB, :]
+            a, b = core_a[part, v, row : row + SUB, :], core_b[part, v, row : row + SUB, :]
             return jnp.where(even_x, b, a)
         if row < halo + rows:
-            return vel[0, v, row - halo : row - halo + SUB, :]
+            return core[part, v, row - halo : row - halo + SUB, :]
         row = row - halo - rows
-        a, b = vel_a[0, v, row : row + SUB, :], vel_b[0, v, row : row + SUB, :]
+        a, b = core_a[part, v, row : row + SUB, :], core_b[part, v, row : row + SUB, :]
         return jnp.where(even_x, a, b)
 
     weights = term_weights(order)
@@ -266,31 +352,6 @@
         lowest_freq + (highest_freq - lowest_freq) * (freq + 0.5) / total
     )
     rate = angular * (depth_interval / (order + 1))
-
-    def apply(seen, t, opening):
-        old, now, new = seen
-        for part in range(plan.parts):
-            at = pad + t * SUB
-            double, across = [], []
-            for v in range(ways):
-                mid = now[part, v, at : at + SUB, :]
-                up = now[part, v, at - 1 : at - 1 + SUB, :]
-                down = now[part, v, at + 1 : at + 1 + SUB, :]
-                two = mid if opening else mid + mid
-                double.append(two)
-                across.append((mid + mid) + (up + down))
-            wrap_low = pltpu.roll(across[-1], 1, 1)
-            wrap_high = pltpu.roll(across[0], LANES - 1, 1)
-            line = [wrap_low] + across + [wrap_high]
-            pairs = [line[i] + line[i + 1] for i in range(ways + 1)]
-            for v in range(ways):
-                total_sum = pairs[v] + pairs[v + 1]
-                if opening:
-                    value = 0.125 * total_sum - double[v]
-                else:
-                    before = old[part, v, at : at + SUB, :]
-                    value = (0.25 * total_sum - double[v]) - before
-                new[part, v, at : at + SUB, :] = grid_edges(value, v, t)
 
     natural = lanes + halo
     source = natural // ways
@@ -331,17 +392,15 @@
                 image[slot, home : home + SUB, :] = tally
 
     for slot, depth in enumerate(depth_list):
-        for t in range(depth, tiles - depth):
-            apply((None, hist.at[0], hist.at[1]), t, True)
-
-        def step(n, carry):
-            view = hist.at[pl.ds(n - 2, 3)]
-            seen = view.at[0], view.at[1], view.at[2]
-            for t in range(depth, tiles - depth):
-                apply(seen, t, False)
-            return carry
-
-        lax.fori_loop(2, order + 1, step, 0)
+        work = [t for t in range(depth, tiles - depth) if depth > 0 or t not in inner]
+        state.terms(hist, order, [(t, pad + t * SUB) for t in work])
+
+        def term(n, part, v, t):
+            at = pad + t * SUB
+            if depth == 0 and t in inner:
+                return known[n, part, v, at - skip : at - skip + SUB, :]
+            return hist[n, part, v, at : at + SUB, :]
+
         final = depth == plan.depths - 1
         spread = depth * span + within
         inside = range(halo // SUB, (halo + rows) // SUB)
@@ -351,11 +410,11 @@
             trig = [small_trig(rate * pick(slowness_at(v, t), spread)) for v in range(ways)]
             twice = [cosine + cosine for _, cosine in trig]
             cells = [(part, v) for v in range(ways) for part in range(plan.parts)]
-            near = [weights[order] * hist[order, p, v, at : at + SUB, :] for p, v in cells]
+            near = [weights[order] * term(order, p, v, t) for p, v in cells]
             far = [None] * len(cells)
             for n in range(order - 1, -1, -1):
                 for i, (p, v) in enumerate(cells):
-                    value = weights[n] * hist[n, p, v, at : at + SUB, :] + twice[v] * near[i]
+                    value = weights[n] * term(n, p, v, t) + twice[v] * near[i]
                     if far[i] is not None:
                         value = value - far[i]
                     near[i], far[i] = value, near[i]
@@ -434,41 +493,44 @@
     )(*ins)
 
 
-def assembled(plan, source, got_a, got_b):
-    parts, rows = source.shape[1], source.shape[2]
-    slab = (parts, plan.ways, plan.halo, LANES)
-    return call(
-        functools.partial(assemble_kernel, plan, "gy", "gx"),
-        [source, got_a, got_b],
-        [(parts, plan.ways, rows, LANES), slab, slab],
-        name="assemble",
-    )
-
-
 def per_device(wavefield, velocity):
     order = ORDER
     plan = Plan(wavefield.shape, velocity.shape[0])
     axes = ("freq", "gx", "gy")
     freq_total = plan.freqs * lax.axis_size("freq")
     pieces = gathered(velocity, "freq")
+    fields = plan.parts + 1
     edge = (plan.parts, plan.rows, LANES)
-    first, second = call(
-        functools.partial(pack_kernel, plan, "gy"), [wavefield], [edge, edge], name="pack"
-    )
-    wave_a, wave_b = swap(first, "gy", 0), swap(second, "gy", 1)
-    edge = (1, plan.rows, LANES)
+    first, second, held, own = call(
+        functools.partial(pack_kernel, plan, "gy"),
+        [wavefield, velocity],
+        [edge, edge, wavefield.shape, velocity.shape],
+        flops=1_000_000,
+        name="pack",
+    )
+    edge = (fields, plan.rows, LANES)
     slowness, first, second = call(
         functools.partial(pack_slowness_kernel, plan, "gy", "freq", len(pieces)),
-        pieces,
-        [(plan.depths, 1, plan.rows, plan.tile), edge, edge],
+        [first, second, own, *pieces[1:]],
+        [(plan.depths, plan.rows, plan.tile), edge, edge],
         name="pack_slowness",
     )
-    wave_a, wave_b, first, second = lax.optimization_barrier((wave_a, wave_b, first, second))
-    slow_a, slow_b = swap(first, "gy", 0), swap(second, "gy", 1)
-    tile, send_a, send_b = assembled(plan, wavefield, wave_a, wave_b)
-    wave = tile, swap(send_a, "gx", 0), swap(send_b, "gx", 1)
-    tile, send_a, send_b = assembled(plan, slowness, slow_a, slow_b)
-    slabs = tile, swap(send_a, "gx", 0), swap(send_b, "gx", 1)
+    got_a, got_b = swap(first, "gy", 0), swap(second, "gy", 1)
+    slab = (fields, plan.ways, plan.halo, LANES)
+    tile, send_a, send_b = call(
+        functools.partial(assemble_kernel, plan, "gy", "gx"),
+        [held, slowness, got_a, got_b],
+        [(fields, plan.ways, plan.rows, LANES), slab, slab],
+        name="assemble",
+    )
+    got_a, got_b = swap(send_a, "gx", 0), swap(send_b, "gx", 1)
+    (known,) = call(
+        functools.partial(inner_kernel, plan, order, axes),
+        [tile],
+        [(order + 1, plan.parts, plan.ways, plan.rows + 2 * SUB, LANES)],
+        flops=10_000_000,
+        name="inner",
+    )
     depths = list(range(plan.depths))
     head, tail = depths[:-1], depths[-1:]
     kept = plan.tall - 2 * SUB * len(head)
@@ -477,7 +539,7 @@
     square = (plan.rows, plan.tile)
     image_head, middle, speed_mid = call(
         functools.partial(migrate_kernel, plan, head, order, axes),
-        [*wave, *slabs],
+        [tile, got_a, got_b, known],
         [(len(head),) + square, (plan.parts, plan.ways, kept, LANES), (plan.ways, need, LANES)],
         [hist],
         flops=30_000_000,

time: 59.9 us -> 56.2 us (0.938)
  starting transfers between devices: 13.9 us -> 9.95 us
    ppermute x8 -> x4, starting transfers between devices: 10.3 us -> 6.31 us  [swap(): return lax.ppermute(value, axis, pairs)]
    ppermute x8 -> x4, waiting for transfers between devices: 11.9 us -> 9.03 us  [swap(): return lax.ppermute(value, axis, pairs)]
    ppermute x1, waiting for transfers between devices: 0.01 us -> 1.73 us  [gathered(): lax.ppermute(sent, axis, [(i, i ^ width) for i in range(count)])]
    ppermute x2, waiting for transfers between devices: 2.78 us -> 3.73 us  [sum_over(): lax.ppermute(value, axis, [(i, i ^ width) for i in range(count)])]
    unnamed x6 -> x4, local copies, waits for them, and re-layouts: 1.94 us -> 1.94 us
  transfers between devices with their start and end apart: 11 -> 7, of which waited for: 6 -> 5; matrix products, arithmetic and copies ran while one was open for 0% -> 0% of each run, Pallas kernels for 11% -> 14%
where the time goes in v3:
time: 56.2 us; the launch traced here: 56 us
  Pallas kernels  28.1 us (50%)
  waiting for transfers between devices  14.5 us (26%)
  starting transfers between devices  9.95 us (18%)
  local copies, waits for them, and re-layouts  1.94 us (3%)
  other arithmetic  0.76 us (1%)
  between operations  0.72 us (1%)
    pallas_call x6, Pallas kernels, call(): pl.pallas_call(kernel, out_shape=[jax.ShapeDtypeStruct(s, jnp.float32) fo...  28.1 us
    ppermute x4, waiting for transfers between devices, swap(): return lax.ppermute(value, axis, pairs)  9.03 us
    ppermute x4, starting transfers between devices, swap(): return lax.ppermute(value, axis, pairs)  6.31 us
    ppermute x2, waiting for transfers between devices, sum_over(): lax.ppermute(value, axis, [(i, i ^ width) for i in range(count)])  3.73 us
    ppermute x2, starting transfers between devices, sum_over(): lax.ppermute(value, axis, [(i, i ^ width) for i in range(count)])  2.09 us
    unnamed x4, local copies, waits for them, and re-layouts  1.94 us
    ppermute x1, waiting for transfers between devices, gathered(): lax.ppermute(sent, axis, [(i, i ^ width) for i in range(count)])  1.73 us
    ppermute x1, starting transfers between devices, gathered(): lax.ppermute(sent, axis, [(i, i ^ width) for i in range(count)])  1.56 us
  transfers between devices with their start and end apart: 7, of which 5 were waited for; matrix products, arithmetic and copies ran while one was open for 0% of the time, Pallas kernels for 14%

profile of v3, /device:TPU:20, one launch (start us, length us, event | category | flops | bytes accessed | tf_op | source)
XLA Modules:
  0.0 56.0 jit_solution(13181584764422772327)
XLA Ops:
  0.6 1.6 %collective-permute-start = (f32[4,64,128]{2,1,0:T(8,128)}, f32[4,64,128]{2,1,0:T(8,128)S(1)}, u32[]{:S(2)}, u32[]{:S(2)}) collective-permute-start(f32[4,64,128]{2,1,0:T(8,128)} %speed.1), channel_id=1, source_target_pairs={{0,16},{16,0},{1,17},{17,1},{2,18},{18,2},{3,19},{19,3},{4,20},{20... | collective-permute-start | bytes 393224 | tf_op jit(solution)/shard_map/ppermute | solution.py:464
  2.2 0.0 copy-start
  2.2 1.0 %copy-done = f32[4,2,128,128]{3,2,1,0:T(8,128)S(1)} copy-done((f32[4,2,128,128]{3,2,1,0:T(8,128)S(1)}, f32[4,2,128,128]{3,2,1,0:T(8,128)}, u32[]{:S(2)}) %copy-start) | copy-done | bytes 524312
  3.2 0.0 copy-start.1
  3.2 0.9 %copy-done.1 = f32[4,64,128]{2,1,0:T(8,128)S(1)} copy-done((f32[4,64,128]{2,1,0:T(8,128)S(1)}, f32[4,64,128]{2,1,0:T(8,128)}, u32[]{:S(2)}) %copy-start.1) | copy-done | bytes 131096
  4.1 0.3 pack.1
  4.4 1.7 %collective-permute-done.refs_3_ = f32[4,64,128]{2,1,0:T(8,128)S(1)} collective-permute-done((f32[4,64,128]{2,1,0:T(8,128)}, f32[4,64,128]{2,1,0:T(8,128)S(1)}, u32[]{:S(2)}, u32[]{:S(2)}) %collective-permute-start) | collective-permute-done | bytes 131104 | tf_op jit(solution)/shard_map/ppermute | solution.py:464
  6.1 0.2 pack_slowness.1
  6.3 1.6 %collective-permute-start.1 = (f32[3,128,128]{2,1,0:T(8,128)S(1)}, f32[3,128,128]{2,1,0:T(8,128)S(1)}, u32[]{:S(2)}, u32[]{:S(2)}) collective-permute-start(f32[3,128,128]{2,1,0:T(8,128)S(1)} %get-tuple-element.22), channel_id=1, source_target_pairs={{0,1},{1,0},{2,3},{3,2},{4,5},{5,4},{6,7},{7,6},{8,9},{9,8},{10,11... | collective-permute-start | bytes 589832 | tf_op jit(solution)/shard_map/ppermute | solution.py:455
  8.0 1.9 %collective-permute-start.2 = (f32[3,128,128]{2,1,0:T(8,128)S(1)}, f32[3,128,128]{2,1,0:T(8,128)S(1)}, u32[]{:S(2)}, u32[]{:S(2)}) collective-permute-start(f32[3,128,128]{2,1,0:T(8,128)S(1)} %get-tuple-element.23), channel_id=1, source_target_pairs={{1,2},{2,1},{5,6},{6,5},{9,10},{10,9},{13,14},{14,13},{17,18},{18,... | collective-permute-start | bytes 589832 | tf_op jit(solution)/shard_map/ppermute | solution.py:455
  9.9 2.3 %collective-permute-done.1.got_a = f32[3,128,128]{2,1,0:T(8,128)S(1)} collective-permute-done((f32[3,128,128]{2,1,0:T(8,128)S(1)}, f32[3,128,128]{2,1,0:T(8,128)S(1)}, u32[]{:S(2)}, u32[]{:S(2)}) %collective-permute-start.1) | collective-permute-done | bytes 196640 | tf_op jit(solution)/shard_map/ppermute | solution.py:455
  12.2 3.3 %collective-permute-done.2.got_b = f32[3,128,128]{2,1,0:T(8,128)S(1)} collective-permute-done((f32[3,128,128]{2,1,0:T(8,128)S(1)}, f32[3,128,128]{2,1,0:T(8,128)S(1)}, u32[]{:S(2)}, u32[]{:S(2)}) %collective-permute-start.2) | collective-permute-done | bytes 196640 | tf_op jit(solution)/shard_map/ppermute | solution.py:455
  15.5 2.3 %assemble.1 = (f32[3,6,128,128]{3,2,1,0:T(8,128)S(1)}, f32[3,6,32,128]{3,2,1,0:T(8,128)S(1)}, f32[3,6,32,128]{3,2,1,0:T(8,128)S(1)}) custom-call(f32[4,2,128,128]{3,2,1,0:T(8,128)S(1)} %get-tuple-element.17.src, f32[4,128,128]{2,1,0:T(8,128)S(1)} %get-tuple-element.21.slow, f32[3,128,128]{2,1,0:T(8,128)S(1)} %collective-permute-done.1.got_a, ...), custom_call_target="tpu_custom_call" | custom-call | bytes 2949120 | tf_op jit(solution)/shard_map/assemble/pallas_call | solution.py:484
  17.8 0.1 collective-permute-start.3
  17.9 2.7 %collective-permute-start.4 = (f32[3,6,32,128]{3,2,1,0:T(8,128)S(1)}, f32[3,6,32,128]{3,2,1,0:T(8,128)S(1)}, u32[]{:S(2)}, u32[]{:S(2)}) collective-permute-start(f32[3,6,32,128]{3,2,1,0:T(8,128)S(1)} %get-tuple-element.26), channel_id=1, source_target_pairs={{4,8},{8,4},{5,9},{9,5},{6,10},{10,6},{7,11},{11,7},{20,24},{24,20... | collective-permute-start | bytes 884744 | tf_op jit(solution)/shard_map/ppermute | solution.py:455
  20.6 1.9 %inner.1.refs_3_ = f32[9,2,6,144,128]{4,3,2,1,0:T(8,128)S(1)} custom-call(f32[3,6,128,128]{3,2,1,0:T(8,128)S(1)} %get-tuple-element.24.tile.refs_0_), custom_call_target="tpu_custom_call" | custom-call | flops 10000000 | bytes 9142272 | tf_op jit(solution)/shard_map/inner/pallas_call | solution.py:484
  22.6 0.0 collective-permute-done.3.refs_1_
  22.6 3.4 %collective-permute-done.4.refs_2_ = f32[3,6,32,128]{3,2,1,0:T(8,128)S(1)} collective-permute-done((f32[3,6,32,128]{3,2,1,0:T(8,128)S(1)}, f32[3,6,32,128]{3,2,1,0:T(8,128)S(1)}, u32[]{:S(2)}, u32[]{:S(2)}) %collective-permute-start.4) | collective-permute-done | bytes 294944 | tf_op jit(solution)/shard_map/ppermute | solution.py:455
  26.0 17.8 %head.1 = (f32[3,128,128]{2,1,0:T(8,128)S(1)}, f32[2,6,144,128]{3,2,1,0:T(8,128)S(1)}, f32[6,128,128]{2,1,0:T(8,128)S(1)}) custom-call(f32[3,6,128,128]{3,2,1,0:T(8,128)S(1)} %get-tuple-element.24.tile.refs_0_, f32[3,6,32,128]{3,2,1,0:T(8,128)S(1)} %collective-permute-done.3.refs_1_, f32[3,6,32,128]{3,2,1,0:T(8,128)S(1)} %collective-permute-done.4.refs_2_, ...), custom_call_target="tpu_custom_call" | custom-call | flops 30000000 | bytes 11206656 | tf_op jit(solution)/shard_map/head/pallas_call | solution.py:484
  43.7 1.6 %collective-permute-start.5 = (f32[3,128,128]{2,1,0:T(8,128)S(1)}, f32[3,128,128]{2,1,0:T(8,128)S(1)}, u32[]{:S(2)}, u32[]{:S(2)}) collective-permute-start(f32[3,128,128]{2,1,0:T(8,128)S(1)} %get-tuple-element.27), channel_id=1, source_target_pairs={{0,16},{16,0},{1,17},{17,1},{2,18},{18,2},{3,19},{19,3},{4,20},{20... | collective-permute-start | bytes 589832 | tf_op jit(solution)/shard_map/ppermute | solution.py:473
  45.3 5.6 %tail.1 = (f32[1,128,128]{2,1,0:T(8,128)S(1)}, f32[4,2,128,128]{3,2,1,0:T(8,128)}) custom-call(f32[2,6,144,128]{3,2,1,0:T(8,128)S(1)} %get-tuple-element.28.refs_0_, f32[6,128,128]{2,1,0:T(8,128)S(1)} %get-tuple-element.29.refs_1_), custom_call_target="tpu_custom_call" | custom-call | flops 30000000 | bytes 1867776 | tf_op jit(solution)/shard_map/tail/pallas_call | solution.py:484
  50.9 0.5 collective-permute-start.6
  51.4 3.7 %collective-permute-done.6 = f32[1,128,128]{2,1,0:T(8,128)S(1)} collective-permute-done((f32[1,128,128]{2,1,0:T(8,128)S(1)}, f32[1,128,128]{2,1,0:T(8,128)S(1)}, u32[]{:S(2)}, u32[]{:S(2)}) %collective-permute-start.6) | collective-permute-done | bytes 65568 | tf_op jit(solution)/shard_map/ppermute | solution.py:473
  55.2 0.0 collective-permute-done.5
  55.2 0.7 %maximum_multiply_fusion = f32[4,128,128]{2,1,0:T(8,128)} fusion(f32[1,128,128]{2,1,0:T(8,128)S(1)} %add.7, f32[3,128,128]{2,1,0:T(8,128)S(1)} %add.6), kind=kLoop, calls=%fused_computation | loop fusion | flops 131072 | bytes 524288 | tf_op jit(solution)/shard_map/mul | solution.py:557
  (2 shorter events, 0.0 us)
Async XLA Ops:
  0.6 5.5 %collective-permute-start = (f32[4,64,128]{2,1,0:T(8,128)}, f32[4,64,128]{2,1,0:T(8,128)S(1)}, u32[]{:S(2)}, u32[]{:S(2)}) collective-permute-start(f32[4,64,128]{2,1,0:T(8,128)} %speed.1), channel_id=1, source_target_pairs={{0,16},{16,0},{1,17},{17,1},{2,18},{18,2},{3,19},{19,3},{4,20},{20... | collective-permute-start | bytes 393224 | tf_op jit(solution)/shard_map/ppermute | solution.py:464
  2.2 1.0 %copy-start = (f32[4,2,128,128]{3,2,1,0:T(8,128)S(1)}, f32[4,2,128,128]{3,2,1,0:T(8,128)}, u32[]{:S(2)}) copy-start(f32[4,2,128,128]{3,2,1,0:T(8,128)} %src.1) | copy-start | bytes 1572868
  3.2 0.9 %copy-start.1 = (f32[4,64,128]{2,1,0:T(8,128)S(1)}, f32[4,64,128]{2,1,0:T(8,128)}, u32[]{:S(2)}) copy-start(f32[4,64,128]{2,1,0:T(8,128)} %speed.1) | copy-start | bytes 393220
  6.3 5.9 %collective-permute-start.1 = (f32[3,128,128]{2,1,0:T(8,128)S(1)}, f32[3,128,128]{2,1,0:T(8,128)S(1)}, u32[]{:S(2)}, u32[]{:S(2)}) collective-permute-start(f32[3,128,128]{2,1,0:T(8,128)S(1)} %get-tuple-element.22), channel_id=1, source_target_pairs={{0,1},{1,0},{2,3},{3,2},{4,5},{5,4},{6,7},{7,6},{8,9},{9,8},{10,11... | collective-permute-start | bytes 589832 | tf_op jit(solution)/shard_map/ppermute | solution.py:455
  8.0 7.6 %collective-permute-start.2 = (f32[3,128,128]{2,1,0:T(8,128)S(1)}, f32[3,128,128]{2,1,0:T(8,128)S(1)}, u32[]{:S(2)}, u32[]{:S(2)}) collective-permute-start(f32[3,128,128]{2,1,0:T(8,128)S(1)} %get-tuple-element.23), channel_id=1, source_target_pairs={{1,2},{2,1},{5,6},{6,5},{9,10},{10,9},{13,14},{14,13},{17,18},{18,... | collective-permute-start | bytes 589832 | tf_op jit(solution)/shard_map/ppermute | solution.py:455
  17.8 4.7 %collective-permute-start.3 = (f32[3,6,32,128]{3,2,1,0:T(8,128)S(1)}, f32[3,6,32,128]{3,2,1,0:T(8,128)S(1)}, u32[]{:S(2)}, u32[]{:S(2)}) collective-permute-start(f32[3,6,32,128]{3,2,1,0:T(8,128)S(1)} %get-tuple-element.25), channel_id=1, source_target_pairs={{0,4},{4,0},{8,12},{12,8},{1,5},{5,1},{9,13},{13,9},{2,6},{6,2},{1... | collective-permute-start | bytes 884744 | tf_op jit(solution)/shard_map/ppermute | solution.py:455
  17.9 8.0 %collective-permute-start.4 = (f32[3,6,32,128]{3,2,1,0:T(8,128)S(1)}, f32[3,6,32,128]{3,2,1,0:T(8,128)S(1)}, u32[]{:S(2)}, u32[]{:S(2)}) collective-permute-start(f32[3,6,32,128]{3,2,1,0:T(8,128)S(1)} %get-tuple-element.26), channel_id=1, source_target_pairs={{4,8},{8,4},{5,9},{9,5},{6,10},{10,6},{7,11},{11,7},{20,24},{24,20... | collective-permute-start | bytes 884744 | tf_op jit(solution)/shard_map/ppermute | solution.py:455
  43.7 11.5 %collective-permute-start.5 = (f32[3,128,128]{2,1,0:T(8,128)S(1)}, f32[3,128,128]{2,1,0:T(8,128)S(1)}, u32[]{:S(2)}, u32[]{:S(2)}) collective-permute-start(f32[3,128,128]{2,1,0:T(8,128)S(1)} %get-tuple-element.27), channel_id=1, source_target_pairs={{0,16},{16,0},{1,17},{17,1},{2,18},{18,2},{3,19},{19,3},{4,20},{20... | collective-permute-start | bytes 589832 | tf_op jit(solution)/shard_map/ppermute | solution.py:473
  50.9 4.3 %collective-permute-start.6 = (f32[1,128,128]{2,1,0:T(8,128)S(1)}, f32[1,128,128]{2,1,0:T(8,128)S(1)}, u32[]{:S(2)}, u32[]{:S(2)}) collective-permute-start(f32[1,128,128]{2,1,0:T(8,128)S(1)} %get-tuple-element.30), channel_id=1, source_target_pairs={{0,16},{16,0},{1,17},{17,1},{2,18},{18,2},{3,19},{19,3},{4,20},{20... | collective-permute-start | bytes 196616 | tf_op jit(solution)/shard_map/ppermute | solution.py:473

commit v4 on v3

--- a/solution.py
+++ b/solution.py
@@ -264,8 +264,78 @@
     return range((plan.halo + SUB) // SUB, (plan.halo + plan.rows - SUB) // SUB)
 
 
-def inner_kernel(plan, order, axes, tile, hist):
+def angle_rate(plan, state, order, axis_f):
+    count = plan.freqs
+    total = count * lax.axis_size(axis_f)
+    freq = (lax.axis_index(axis_f) * count + state.which).astype(jnp.float32)
+    angular = (2.0 * math.pi) * (
+        lowest_freq + (highest_freq - lowest_freq) * (freq + 0.5) / total
+    )
+    return angular * (depth_interval / (order + 1))
+
+
+def sum_terms(plan, state, order, rate, depth, slow, term, store):
+    ways, weights = plan.ways, term_weights(order)
+    spread = depth * plan.span + state.within
+    trig = [small_trig(rate * pick(slow(v), spread)) for v in range(ways)]
+    twice = [cosine + cosine for _, cosine in trig]
+    cells = [(part, v) for v in range(ways) for part in range(plan.parts)]
+    near = [weights[order] * term(order, p, v) for p, v in cells]
+    far = [None] * len(cells)
+    for n in range(order - 1, -1, -1):
+        for i, (p, v) in enumerate(cells):
+            value = weights[n] * term(n, p, v) + twice[v] * near[i]
+            if far[i] is not None:
+                value = value - far[i]
+            near[i], far[i] = value, near[i]
+    for v in range(ways):
+        sine, cosine = trig[v]
+        real, imag = plan.parts * v, plan.parts * v + 1
+        store(0, v, cosine * near[real] - sine * near[imag] - far[real])
+        store(1, v, sine * near[real] + cosine * near[imag] - far[imag])
+
+
+def picture(plan, state, real):
+    natural = state.lanes + plan.halo
+    source = natural // plan.ways
+    step_of = natural - source * plan.ways
+    tally = None
+    for v in range(plan.ways):
+        fold = real(v)
+        width = LANES // 2
+        while width >= plan.span:
+            fold = fold + pltpu.roll(fold, width, 1)
+            width //= 2
+        fold = pick(fold, source)
+        tally = fold if tally is None else jnp.where(step_of == v, fold, tally)
+    return tally
+
+
+def unpack_kernel(plan, fresh, out):
+    lanes = lane_iota()
+    index, owner = [], []
+    for v in range(plan.ways):
+        where = jnp.zeros_like(lanes)
+        for f in range(plan.freqs):
+            column, mine = taken(plan, lanes, v, f)
+            where = jnp.where(mine, f * plan.span + column // plan.ways, where)
+        index.append(where)
+    for f in range(plan.freqs):
+        owner.append(lax.rem(taken(plan, lanes, 0, f)[0], plan.ways))
+    for part in range(plan.parts):
+        for row in range(0, plan.rows, SUB):
+            here = slice(row, row + SUB)
+            found = [pick(fresh[part, v, here, :], index[v]) for v in range(plan.ways)]
+            for f in range(plan.freqs):
+                value = found[0]
+                for v in range(1, plan.ways):
+                    value = jnp.where(owner[f] == v, found[v], value)
+                out[f, part, here, :] = turn(value, -plan.offsets[f])
+
+
+def inner_kernel(plan, order, axes, tile, fresh, rim, shot, hist):
     state = Tile(plan, axes)
+    rate = angle_rate(plan, state, order, axes[0])
     for part in range(plan.parts):
         for v in range(plan.ways):
             for row in range(0, plan.rows, SUB):
@@ -273,6 +343,31 @@
     first = plan.halo // SUB
     rows = [(first + i, SUB + i * SUB) for i in range(plan.rows // SUB)]
     state.terms(hist, order, rows)
+    inner = inner_tiles(plan)
+    for t in inner:
+        home = t * SUB - plan.halo
+        at, to = home + SUB, (t - inner[0]) * SUB
+
+        def store(part, v, value):
+            fresh[part, v, to : to + SUB, :] = value
+
+        sum_terms(
+            plan,
+            state,
+            order,
+            rate,
+            0,
+            lambda v: tile[plan.parts, v, home : home + SUB, :],
+            lambda n, p, v: hist[n, p, v, at : at + SUB, :],
+            store,
+        )
+        shot[to : to + SUB, :] = picture(plan, state, lambda v: fresh[0, v, to : to + SUB, :])
+    for side, t in enumerate((inner[0], inner[-1])):
+        at = t * SUB - plan.halo + SUB
+        for n in range(1, order):
+            for part in range(plan.parts):
+                for v in range(plan.ways):
+                    rim[n, side, part, v] = hist[n, part, v, at : at + SUB, :]
 
 
 def migrate_kernel(plan, depth_list, order, axes, *refs):
@@ -281,8 +376,8 @@
     last = depth_list[-1] == plan.depths - 1
     refs = list(refs)
     if first:
-        core, core_a, core_b, known = refs[:4]
-        refs = refs[4:]
+        core, core_a, core_b, fresh, rim, shot = refs[:6]
+        refs = refs[6:]
     else:
         start, vel = refs[:2]
         refs = refs[2:]
@@ -298,7 +393,6 @@
     state = Tile(plan, axes)
     even_x, lanes, which, within = state.even_x, state.lanes, state.which, state.within
     inner = inner_tiles(plan)
-    skip = halo
 
     if first:
         for part in range(plan.parts):
@@ -314,12 +408,10 @@
                         continue
                     at, row = pad + t * SUB, t * SUB - halo
                     hist[0, part, v, at : at + SUB, :] = core[part, v, row : row + SUB, :]
-                for t in (inner[0], inner[-1]):
+                for side, t in enumerate((inner[0], inner[-1])):
                     at = pad + t * SUB
                     for n in range(1, order):
-                        hist[n, part, v, at : at + SUB, :] = known[
-                            n, part, v, at - skip : at - skip + SUB, :
-                        ]
+                        hist[n, part, v, at : at + SUB, :] = rim[n, side, part, v]
     else:
         lead = SUB * depth_list[0]
         for part in range(plan.parts):
@@ -344,100 +436,46 @@
         a, b = core_a[part, v, row : row + SUB, :], core_b[part, v, row : row + SUB, :]
         return jnp.where(even_x, a, b)
 
-    weights = term_weights(order)
-    count = plan.freqs
-    total = count * lax.axis_size(axis_f)
-    freq = (lax.axis_index(axis_f) * count + which).astype(jnp.float32)
-    angular = (2.0 * math.pi) * (
-        lowest_freq + (highest_freq - lowest_freq) * (freq + 0.5) / total
-    )
-    rate = angular * (depth_interval / (order + 1))
-
-    natural = lanes + halo
-    source = natural // ways
-    step_of = natural - source * ways
-
-    def convert(t, slot, final):
-        at, home = pad + t * SUB, t * SUB - halo
-        if not final:
-            tally = None
-            for v in range(ways):
-                fold = hist[0, 0, v, at : at + SUB, :]
-                width = LANES // 2
-                while width >= span:
-                    fold = fold + pltpu.roll(fold, width, 1)
-                    width //= 2
-                fold = pick(fold, source)
-                tally = fold if tally is None else jnp.where(step_of == v, fold, tally)
-            image[slot, home : home + SUB, :] = tally
-            return
-        for part in range(plan.parts):
-            spread_out = []
-            for v in range(ways):
-                index = jnp.zeros_like(lanes)
-                for f in range(plan.freqs):
-                    column, mine = taken(plan, lanes, v, f)
-                    index = jnp.where(mine, f * span + column // ways, index)
-                spread_out.append(pick(hist[0, part, v, at : at + SUB, :], index))
-            tally = None
-            for f in range(plan.freqs):
-                value = spread_out[0]
-                for v in range(1, ways):
-                    value = jnp.where(taken(plan, lanes, v, f)[1], spread_out[v], value)
-                value = turn(value, -plan.offsets[f])
-                out[f, part, home : home + SUB, :] = value
-                if part == 0:
-                    tally = value if tally is None else tally + value
-            if part == 0:
-                image[slot, home : home + SUB, :] = tally
-
+    rate = angle_rate(plan, state, order, axis_f)
+    inside = range(halo // SUB, (halo + rows) // SUB)
     for slot, depth in enumerate(depth_list):
         work = [t for t in range(depth, tiles - depth) if depth > 0 or t not in inner]
         state.terms(hist, order, [(t, pad + t * SUB) for t in work])
-
-        def term(n, part, v, t):
-            at = pad + t * SUB
+        leaving = depth == depth_list[-1]
+        lead = SUB * (depth + 1)
+        for t in range(depth + 1, tiles - depth - 1):
             if depth == 0 and t in inner:
-                return known[n, part, v, at - skip : at - skip + SUB, :]
-            return hist[n, part, v, at : at + SUB, :]
-
-        final = depth == plan.depths - 1
-        spread = depth * span + within
-        inside = range(halo // SUB, (halo + rows) // SUB)
-        waiting = []
-        for t in range(depth + 1, tiles - depth - 1):
-            at = pad + t * SUB
-            trig = [small_trig(rate * pick(slowness_at(v, t), spread)) for v in range(ways)]
-            twice = [cosine + cosine for _, cosine in trig]
-            cells = [(part, v) for v in range(ways) for part in range(plan.parts)]
-            near = [weights[order] * term(order, p, v, t) for p, v in cells]
-            far = [None] * len(cells)
-            for n in range(order - 1, -1, -1):
-                for i, (p, v) in enumerate(cells):
-                    value = weights[n] * term(n, p, v, t) + twice[v] * near[i]
-                    if far[i] is not None:
-                        value = value - far[i]
-                    near[i], far[i] = value, near[i]
-            for v in range(ways):
-                sine, cosine = trig[v]
-                real, imag = plan.parts * v, plan.parts * v + 1
-                new_real = cosine * near[real] - sine * near[imag] - far[real]
-                new_imag = sine * near[real] + cosine * near[imag] - far[imag]
-                hist[0, 0, v, at : at + SUB, :] = new_real
-                hist[0, 1, v, at : at + SUB, :] = new_imag
+                continue
+            at, to, home = pad + t * SUB, t * SUB - lead, t * SUB - halo
+
+            def store(part, v, value):
+                if leaving:
+                    out[part, v, to : to + SUB, :] = value
+                else:
+                    hist[0, part, v, at : at + SUB, :] = value
+
+            def real(v):
+                return out[0, v, to : to + SUB, :] if leaving else hist[0, 0, v, at : at + SUB, :]
+
+            sum_terms(
+                plan,
+                state,
+                order,
+                rate,
+                depth,
+                lambda v: slowness_at(v, t),
+                lambda n, p, v: hist[n, p, v, at : at + SUB, :],
+                store,
+            )
             if t in inside:
-                waiting.append(t)
-            if len(waiting) > 1:
-                convert(waiting.pop(0), slot, final)
-        for t in waiting:
-            convert(t, slot, final)
-    if not last:
-        lead = SUB * (depth_list[-1] + 1)
-        for part in range(plan.parts):
-            for v in range(ways):
-                for row in range(lead, plan.tall - lead, SUB):
-                    at = pad + row
-                    out[part, v, row - lead : row - lead + SUB, :] = hist[0, part, v, at : at + SUB, :]
+                image[slot, home : home + SUB, :] = picture(plan, state, real)
+        if depth == 0:
+            for t in inner:
+                at, to, home = pad + t * SUB, (t - inner[0]) * SUB, t * SUB - halo
+                image[slot, home : home + SUB, :] = shot[to : to + SUB, :]
+                for part in range(plan.parts):
+                    for v in range(ways):
+                        hist[0, part, v, at : at + SUB, :] = fresh[part, v, to : to + SUB, :]
     if first and not last:
         lead = SUB * (depth_list[-1] + 2)
         for v in range(ways):
@@ -524,10 +562,16 @@
         name="assemble",
     )
     got_a, got_b = swap(send_a, "gx", 0), swap(send_b, "gx", 1)
-    (known,) = call(
+    held_rows = SUB * len(inner_tiles(plan))
+    fresh, rim, shot = call(
         functools.partial(inner_kernel, plan, order, axes),
         [tile],
-        [(order + 1, plan.parts, plan.ways, plan.rows + 2 * SUB, LANES)],
+        [
+            (plan.parts, plan.ways, held_rows, LANES),
+            (order, 2, plan.parts, plan.ways, SUB, LANES),
+            (held_rows, plan.tile),
+        ],
+        [pltpu.VMEM((order + 1, plan.parts, plan.ways, plan.rows + 2 * SUB, LANES), jnp.float32)],
         flops=10_000_000,
         name="inner",
     )
@@ -539,7 +583,7 @@
     square = (plan.rows, plan.tile)
     image_head, middle, speed_mid = call(
         functools.partial(migrate_kernel, plan, head, order, axes),
-        [tile, got_a, got_b, known],
+        [tile, got_a, got_b, fresh, rim, shot],
         [(len(head),) + square, (plan.parts, plan.ways, kept, LANES), (plan.ways, need, LANES)],
         [hist],
         flops=30_000_000,
@@ -548,10 +592,17 @@
     image_tail, last = call(
         functools.partial(migrate_kernel, plan, tail, order, axes),
         [middle, speed_mid],
-        [(len(tail),) + square, wavefield.shape],
+        [(len(tail),) + square, (plan.parts, plan.ways, plan.rows, LANES)],
         [hist],
         flops=30_000_000,
         name="tail",
+    )
+    (last,) = call(
+        functools.partial(unpack_kernel, plan),
+        [last],
+        [wavefield.shape],
+        flops=5_000_000,
+        name="unpack",
     )
     scale = 1.0 / math.sqrt(freq_total)
     image = jnp.concatenate([sum_over(image_head, "freq"), sum_over(image_tail, "freq")]) * scale

time: 56.2 us -> 53.8 us (0.957)
  waiting for transfers between devices: 14.5 us -> 9.7 us
  Pallas kernels: 28.1 us -> 30.5 us
    ppermute x2, waiting for transfers between devices: 3.73 us -> 0.88 us  [sum_over(): lax.ppermute(value, axis, [(i, i ^ width) for i in range(count)])]
    pallas_call x6 -> x7, Pallas kernels: 28.1 us -> 30.5 us  [call(): pl.pallas_call(kernel, out_shape=[jax.ShapeDtypeStruct(s, jnp.float32) fo...]
    ppermute x4, waiting for transfers between devices: 9.03 us -> 7.09 us  [swap(): return lax.ppermute(value, axis, pairs)]
  transfers between devices with their start and end apart: 7 -> 7, of which waited for: 5 -> 5; matrix products, arithmetic and copies ran while one was open for 0% -> 0% of each run, Pallas kernels for 14% -> 23%
where the time goes in v4:
time: 53.8 us; the launch traced here: 53.6 us
  Pallas kernels  30.5 us (57%)
  starting transfers between devices  9.97 us (19%)
  waiting for transfers between devices  9.7 us (18%)
  local copies, waits for them, and re-layouts  1.94 us (4%)
  other arithmetic  0.76 us (1%)
  between operations  0.72 us (1%)
    pallas_call x7, Pallas kernels, call(): pl.pallas_call(kernel, out_shape=[jax.ShapeDtypeStruct(s, jnp.float32) fo...  30.5 us
    ppermute x4, waiting for transfers between devices, swap(): return lax.ppermute(value, axis, pairs)  7.09 us
    ppermute x4, starting transfers between devices, swap(): return lax.ppermute(value, axis, pairs)  6.31 us
    ppermute x2, starting transfers between devices, sum_over(): lax.ppermute(value, axis, [(i, i ^ width) for i in range(count)])  2.11 us
    unnamed x4, local copies, waits for them, and re-layouts  1.94 us
    ppermute x1, waiting for transfers between devices, gathered(): lax.ppermute(sent, axis, [(i, i ^ width) for i in range(count)])  1.73 us
    ppermute x1, starting transfers between devices, gathered(): lax.ppermute(sent, axis, [(i, i ^ width) for i in range(count)])  1.56 us
  transfers between devices with their start and end apart: 7, of which 5 were waited for; matrix products, arithmetic and copies ran while one was open for 0% of the time, Pallas kernels for 23%

profile of v4, /device:TPU:20, one launch (start us, length us, event | category | flops | bytes accessed | tf_op | source)
XLA Modules:
  0.0 53.6 jit_solution(10749638964019257703)
XLA Ops:
  0.6 1.6 %collective-permute-start = (f32[4,64,128]{2,1,0:T(8,128)}, f32[4,64,128]{2,1,0:T(8,128)S(1)}, u32[]{:S(2)}, u32[]{:S(2)}) collective-permute-start(f32[4,64,128]{2,1,0:T(8,128)} %speed.1), channel_id=1, source_target_pairs={{0,16},{16,0},{1,17},{17,1},{2,18},{18,2},{3,19},{19,3},{4,20},{20... | collective-permute-start | bytes 393224 | tf_op jit(solution)/shard_map/ppermute | solution.py:502
  2.2 0.0 copy-start
  2.2 1.0 %copy-done = f32[4,2,128,128]{3,2,1,0:T(8,128)S(1)} copy-done((f32[4,2,128,128]{3,2,1,0:T(8,128)S(1)}, f32[4,2,128,128]{3,2,1,0:T(8,128)}, u32[]{:S(2)}) %copy-start) | copy-done | bytes 524312
  3.2 0.0 copy-start.1
  3.2 0.9 %copy-done.1 = f32[4,64,128]{2,1,0:T(8,128)S(1)} copy-done((f32[4,64,128]{2,1,0:T(8,128)S(1)}, f32[4,64,128]{2,1,0:T(8,128)}, u32[]{:S(2)}) %copy-start.1) | copy-done | bytes 131096
  4.1 0.3 pack.1
  4.4 1.7 %collective-permute-done.refs_3_ = f32[4,64,128]{2,1,0:T(8,128)S(1)} collective-permute-done((f32[4,64,128]{2,1,0:T(8,128)}, f32[4,64,128]{2,1,0:T(8,128)S(1)}, u32[]{:S(2)}, u32[]{:S(2)}) %collective-permute-start) | collective-permute-done | bytes 131104 | tf_op jit(solution)/shard_map/ppermute | solution.py:502
  6.1 0.2 pack_slowness.1
  6.3 1.6 %collective-permute-start.1 = (f32[3,128,128]{2,1,0:T(8,128)S(1)}, f32[3,128,128]{2,1,0:T(8,128)S(1)}, u32[]{:S(2)}, u32[]{:S(2)}) collective-permute-start(f32[3,128,128]{2,1,0:T(8,128)S(1)} %get-tuple-element.25), channel_id=1, source_target_pairs={{0,1},{1,0},{2,3},{3,2},{4,5},{5,4},{6,7},{7,6},{8,9},{9,8},{10,11... | collective-permute-start | bytes 589832 | tf_op jit(solution)/shard_map/ppermute | solution.py:493
  8.0 1.9 %collective-permute-start.2 = (f32[3,128,128]{2,1,0:T(8,128)S(1)}, f32[3,128,128]{2,1,0:T(8,128)S(1)}, u32[]{:S(2)}, u32[]{:S(2)}) collective-permute-start(f32[3,128,128]{2,1,0:T(8,128)S(1)} %get-tuple-element.26), channel_id=1, source_target_pairs={{1,2},{2,1},{5,6},{6,5},{9,10},{10,9},{13,14},{14,13},{17,18},{18,... | collective-permute-start | bytes 589832 | tf_op jit(solution)/shard_map/ppermute | solution.py:493
  9.9 2.3 %collective-permute-done.1.got_a = f32[3,128,128]{2,1,0:T(8,128)S(1)} collective-permute-done((f32[3,128,128]{2,1,0:T(8,128)S(1)}, f32[3,128,128]{2,1,0:T(8,128)S(1)}, u32[]{:S(2)}, u32[]{:S(2)}) %collective-permute-start.1) | collective-permute-done | bytes 196640 | tf_op jit(solution)/shard_map/ppermute | solution.py:493
  12.2 3.3 %collective-permute-done.2.got_b = f32[3,128,128]{2,1,0:T(8,128)S(1)} collective-permute-done((f32[3,128,128]{2,1,0:T(8,128)S(1)}, f32[3,128,128]{2,1,0:T(8,128)S(1)}, u32[]{:S(2)}, u32[]{:S(2)}) %collective-permute-start.2) | collective-permute-done | bytes 196640 | tf_op jit(solution)/shard_map/ppermute | solution.py:493
  15.5 2.3 %assemble.1 = (f32[3,6,128,128]{3,2,1,0:T(8,128)S(1)}, f32[3,6,32,128]{3,2,1,0:T(8,128)S(1)}, f32[3,6,32,128]{3,2,1,0:T(8,128)S(1)}) custom-call(f32[4,2,128,128]{3,2,1,0:T(8,128)S(1)} %get-tuple-element.20.src, f32[4,128,128]{2,1,0:T(8,128)S(1)} %get-tuple-element.24.slow, f32[3,128,128]{2,1,0:T(8,128)S(1)} %collective-permute-done.1.got_a, ...), custom_call_target="tpu_custom_call" | custom-call | bytes 2949120 | tf_op jit(solution)/shard_map/assemble/pallas_call | solution.py:522
  17.8 0.1 collective-permute-start.3
  17.9 2.7 %collective-permute-start.4 = (f32[3,6,32,128]{3,2,1,0:T(8,128)S(1)}, f32[3,6,32,128]{3,2,1,0:T(8,128)S(1)}, u32[]{:S(2)}, u32[]{:S(2)}) collective-permute-start(f32[3,6,32,128]{3,2,1,0:T(8,128)S(1)} %get-tuple-element.29), channel_id=1, source_target_pairs={{4,8},{8,4},{5,9},{9,5},{6,10},{10,6},{7,11},{11,7},{20,24},{24,20... | collective-permute-start | bytes 884744 | tf_op jit(solution)/shard_map/ppermute | solution.py:493
  20.6 3.9 %inner.1 = (f32[2,6,112,128]{3,2,1,0:T(8,128)S(1)}, f32[8,2,2,6,8,128]{5,4,3,2,1,0:T(8,128)S(1)}, f32[112,128]{1,0:T(8,128)S(1)}) custom-call(f32[3,6,128,128]{3,2,1,0:T(8,128)S(1)} %get-tuple-element.27.tile.refs_0_), custom_call_target="tpu_custom_call" | custom-call | flops 10000000 | bytes 2711552 | tf_op jit(solution)/shard_map/inner/pallas_call | solution.py:522
  24.5 0.0 collective-permute-done.3.refs_1_
  24.5 1.5 %collective-permute-done.4.refs_2_ = f32[3,6,32,128]{3,2,1,0:T(8,128)S(1)} collective-permute-done((f32[3,6,32,128]{3,2,1,0:T(8,128)S(1)}, f32[3,6,32,128]{3,2,1,0:T(8,128)S(1)}, u32[]{:S(2)}, u32[]{:S(2)}) %collective-permute-start.4) | collective-permute-done | bytes 294944 | tf_op jit(solution)/shard_map/ppermute | solution.py:493
  26.0 15.7 %head.1 = (f32[3,128,128]{2,1,0:T(8,128)S(1)}, f32[2,6,144,128]{3,2,1,0:T(8,128)S(1)}, f32[6,128,128]{2,1,0:T(8,128)S(1)}) custom-call(f32[3,6,128,128]{3,2,1,0:T(8,128)S(1)} %get-tuple-element.27.tile.refs_0_, f32[3,6,32,128]{3,2,1,0:T(8,128)S(1)} %collective-permute-done.3.refs_1_, f32[3,6,32,128]{3,2,1,0:T(8,128)S(1)} %collective-permute-done.4.refs_2_, ...), custom_call_target="tpu_custom_call" | custom-call | flops 30000000 | bytes 4775936 | tf_op jit(solution)/shard_map/head/pallas_call | solution.py:522
  41.7 1.5 %collective-permute-start.5 = (f32[3,128,128]{2,1,0:T(8,128)S(1)}, f32[3,128,128]{2,1,0:T(8,128)S(1)}, u32[]{:S(2)}, u32[]{:S(2)}) collective-permute-start(f32[3,128,128]{2,1,0:T(8,128)S(1)} %get-tuple-element.33), channel_id=1, source_target_pairs={{0,16},{16,0},{1,17},{17,1},{2,18},{18,2},{3,19},{19,3},{4,20},{20... | collective-permute-start | bytes 589832 | tf_op jit(solution)/shard_map/ppermute | solution.py:511
  43.2 5.2 %tail.1 = (f32[1,128,128]{2,1,0:T(8,128)S(1)}, f32[2,6,128,128]{3,2,1,0:T(8,128)S(1)}) custom-call(f32[2,6,144,128]{3,2,1,0:T(8,128)S(1)} %get-tuple-element.34.refs_0_, f32[6,128,128]{2,1,0:T(8,128)S(1)} %get-tuple-element.35.refs_1_), custom_call_target="tpu_custom_call" | custom-call | flops 30000000 | bytes 2129920 | tf_op jit(solution)/shard_map/tail/pallas_call | solution.py:522
  48.5 0.6 %collective-permute-start.6 = (f32[1,128,128]{2,1,0:T(8,128)S(1)}, f32[1,128,128]{2,1,0:T(8,128)S(1)}, u32[]{:S(2)}, u32[]{:S(2)}) collective-permute-start(f32[1,128,128]{2,1,0:T(8,128)S(1)} %get-tuple-element.36), channel_id=1, source_target_pairs={{0,16},{16,0},{1,17},{17,1},{2,18},{18,2},{3,19},{19,3},{4,20},{20... | collective-permute-start | bytes 196616 | tf_op jit(solution)/shard_map/ppermute | solution.py:511
  49.1 2.9 %unpack.1 = f32[4,2,128,128]{3,2,1,0:T(8,128)} custom-call(f32[2,6,128,128]{3,2,1,0:T(8,128)S(1)} %get-tuple-element.37.fresh), custom_call_target="tpu_custom_call" | custom-call | flops 5000000 | bytes 1310720 | tf_op jit(solution)/shard_map/unpack/pallas_call | solution.py:522
  51.9 0.9 %collective-permute-done.6 = f32[1,128,128]{2,1,0:T(8,128)S(1)} collective-permute-done((f32[1,128,128]{2,1,0:T(8,128)S(1)}, f32[1,128,128]{2,1,0:T(8,128)S(1)}, u32[]{:S(2)}, u32[]{:S(2)}) %collective-permute-start.6) | collective-permute-done | bytes 65568 | tf_op jit(solution)/shard_map/ppermute | solution.py:511
  52.8 0.0 collective-permute-done.5
  52.8 0.7 %maximum_multiply_fusion = f32[4,128,128]{2,1,0:T(8,128)} fusion(f32[1,128,128]{2,1,0:T(8,128)S(1)} %add.7, f32[3,128,128]{2,1,0:T(8,128)S(1)} %add.6), kind=kLoop, calls=%fused_computation | loop fusion | flops 131072 | bytes 524288 | tf_op jit(solution)/shard_map/mul | solution.py:608
  (2 shorter events, 0.0 us)
Async XLA Ops:
  0.6 5.5 %collective-permute-start = (f32[4,64,128]{2,1,0:T(8,128)}, f32[4,64,128]{2,1,0:T(8,128)S(1)}, u32[]{:S(2)}, u32[]{:S(2)}) collective-permute-start(f32[4,64,128]{2,1,0:T(8,128)} %speed.1), channel_id=1, source_target_pairs={{0,16},{16,0},{1,17},{17,1},{2,18},{18,2},{3,19},{19,3},{4,20},{20... | collective-permute-start | bytes 393224 | tf_op jit(solution)/shard_map/ppermute | solution.py:502
  2.2 1.0 %copy-start = (f32[4,2,128,128]{3,2,1,0:T(8,128)S(1)}, f32[4,2,128,128]{3,2,1,0:T(8,128)}, u32[]{:S(2)}) copy-start(f32[4,2,128,128]{3,2,1,0:T(8,128)} %src.1) | copy-start | bytes 1572868
  3.2 0.9 %copy-start.1 = (f32[4,64,128]{2,1,0:T(8,128)S(1)}, f32[4,64,128]{2,1,0:T(8,128)}, u32[]{:S(2)}) copy-start(f32[4,64,128]{2,1,0:T(8,128)} %speed.1) | copy-start | bytes 393220
  6.3 5.9 %collective-permute-start.1 = (f32[3,128,128]{2,1,0:T(8,128)S(1)}, f32[3,128,128]{2,1,0:T(8,128)S(1)}, u32[]{:S(2)}, u32[]{:S(2)}) collective-permute-start(f32[3,128,128]{2,1,0:T(8,128)S(1)} %get-tuple-element.25), channel_id=1, source_target_pairs={{0,1},{1,0},{2,3},{3,2},{4,5},{5,4},{6,7},{7,6},{8,9},{9,8},{10,11... | collective-permute-start | bytes 589832 | tf_op jit(solution)/shard_map/ppermute | solution.py:493
  8.0 7.6 %collective-permute-start.2 = (f32[3,128,128]{2,1,0:T(8,128)S(1)}, f32[3,128,128]{2,1,0:T(8,128)S(1)}, u32[]{:S(2)}, u32[]{:S(2)}) collective-permute-start(f32[3,128,128]{2,1,0:T(8,128)S(1)} %get-tuple-element.26), channel_id=1, source_target_pairs={{1,2},{2,1},{5,6},{6,5},{9,10},{10,9},{13,14},{14,13},{17,18},{18,... | collective-permute-start | bytes 589832 | tf_op jit(solution)/shard_map/ppermute | solution.py:493
  17.8 6.7 %collective-permute-start.3 = (f32[3,6,32,128]{3,2,1,0:T(8,128)S(1)}, f32[3,6,32,128]{3,2,1,0:T(8,128)S(1)}, u32[]{:S(2)}, u32[]{:S(2)}) collective-permute-start(f32[3,6,32,128]{3,2,1,0:T(8,128)S(1)} %get-tuple-element.28), channel_id=1, source_target_pairs={{0,4},{4,0},{8,12},{12,8},{1,5},{5,1},{9,13},{13,9},{2,6},{6,2},{1... | collective-permute-start | bytes 884744 | tf_op jit(solution)/shard_map/ppermute | solution.py:493
  17.9 8.0 %collective-permute-start.4 = (f32[3,6,32,128]{3,2,1,0:T(8,128)S(1)}, f32[3,6,32,128]{3,2,1,0:T(8,128)S(1)}, u32[]{:S(2)}, u32[]{:S(2)}) collective-permute-start(f32[3,6,32,128]{3,2,1,0:T(8,128)S(1)} %get-tuple-element.29), channel_id=1, source_target_pairs={{4,8},{8,4},{5,9},{9,5},{6,10},{10,6},{7,11},{11,7},{20,24},{24,20... | collective-permute-start | bytes 884744 | tf_op jit(solution)/shard_map/ppermute | solution.py:493
  41.7 11.1 %collective-permute-start.5 = (f32[3,128,128]{2,1,0:T(8,128)S(1)}, f32[3,128,128]{2,1,0:T(8,128)S(1)}, u32[]{:S(2)}, u32[]{:S(2)}) collective-permute-start(f32[3,128,128]{2,1,0:T(8,128)S(1)} %get-tuple-element.33), channel_id=1, source_target_pairs={{0,16},{16,0},{1,17},{17,1},{2,18},{18,2},{3,19},{19,3},{4,20},{20... | collective-permute-start | bytes 589832 | tf_op jit(solution)/shard_map/ppermute | solution.py:511
  48.5 4.3 %collective-permute-start.6 = (f32[1,128,128]{2,1,0:T(8,128)S(1)}, f32[1,128,128]{2,1,0:T(8,128)S(1)}, u32[]{:S(2)}, u32[]{:S(2)}) collective-permute-start(f32[1,128,128]{2,1,0:T(8,128)S(1)} %get-tuple-element.36), channel_id=1, source_target_pairs={{0,16},{16,0},{1,17},{17,1},{2,18},{18,2},{3,19},{19,3},{4,20},{20... | collective-permute-start | bytes 196616 | tf_op jit(solution)/shard_map/ppermute | solution.py:511

commit v5 on v4

--- a/solution.py
+++ b/solution.py
@@ -8,6 +8,7 @@
 from jax.experimental import pallas as pl
 from jax.experimental.pallas import tpu as pltpu
 from jax.sharding import PartitionSpec as P
+
 
 ORDER = 8
 LANES = 128
@@ -387,11 +388,11 @@
         vel_out = refs[0]
         refs = refs[1:]
     hist = refs[0]
-    halo, rows, ways, span = plan.halo, plan.rows, plan.ways, plan.span
+    halo, rows, ways = plan.halo, plan.rows, plan.ways
     pad = SUB
     tiles = plan.tall // SUB
     state = Tile(plan, axes)
-    even_x, lanes, which, within = state.even_x, state.lanes, state.which, state.within
+    even_x = state.even_x
     inner = inner_tiles(plan)
 
     if first:
@@ -516,7 +517,7 @@
 VMEM = pl.BlockSpec(memory_space=pltpu.VMEM)
 
 
-def call(kernel, ins, outs, scratch=(), flops=0, name=None):
+def call(kernel, ins, outs, scratch=(), flops=0):
     moved = sum(4 * math.prod(x.shape) for x in ins) + sum(4 * math.prod(s) for s in outs)
     held = moved + sum(4 * math.prod(x.shape) for x in scratch)
     return pl.pallas_call(
@@ -527,11 +528,10 @@
         scratch_shapes=list(scratch),
         cost_estimate=pl.CostEstimate(flops=flops, bytes_accessed=moved, transcendentals=0),
         compiler_params=pltpu.CompilerParams(vmem_limit_bytes=held + (4 << 20)),
-        name=name,
     )(*ins)
 
 
-def per_device(wavefield, velocity):
+def migrated(wavefield, velocity):
     order = ORDER
     plan = Plan(wavefield.shape, velocity.shape[0])
     axes = ("freq", "gx", "gy")
@@ -544,14 +544,12 @@
         [wavefield, velocity],
         [edge, edge, wavefield.shape, velocity.shape],
         flops=1_000_000,
-        name="pack",
     )
     edge = (fields, plan.rows, LANES)
     slowness, first, second = call(
         functools.partial(pack_slowness_kernel, plan, "gy", "freq", len(pieces)),
         [first, second, own, *pieces[1:]],
         [(plan.depths, plan.rows, plan.tile), edge, edge],
-        name="pack_slowness",
     )
     got_a, got_b = swap(first, "gy", 0), swap(second, "gy", 1)
     slab = (fields, plan.ways, plan.halo, LANES)
@@ -559,9 +557,9 @@
         functools.partial(assemble_kernel, plan, "gy", "gx"),
         [held, slowness, got_a, got_b],
         [(fields, plan.ways, plan.rows, LANES), slab, slab],
-        name="assemble",
-    )
-    got_a, got_b = swap(send_a, "gx", 0), swap(send_b, "gx", 1)
+    )
+    got_a = swap(send_a, "gx", 0)
+    got_b = swap(send_b, "gx", 1)
     held_rows = SUB * len(inner_tiles(plan))
     fresh, rim, shot = call(
         functools.partial(inner_kernel, plan, order, axes),
@@ -573,7 +571,6 @@
         ],
         [pltpu.VMEM((order + 1, plan.parts, plan.ways, plan.rows + 2 * SUB, LANES), jnp.float32)],
         flops=10_000_000,
-        name="inner",
     )
     depths = list(range(plan.depths))
     head, tail = depths[:-1], depths[-1:]
@@ -587,7 +584,6 @@
         [(len(head),) + square, (plan.parts, plan.ways, kept, LANES), (plan.ways, need, LANES)],
         [hist],
         flops=30_000_000,
-        name="head",
     )
     image_tail, last = call(
         functools.partial(migrate_kernel, plan, tail, order, axes),
@@ -595,14 +591,9 @@
         [(len(tail),) + square, (plan.parts, plan.ways, plan.rows, LANES)],
         [hist],
         flops=30_000_000,
-        name="tail",
     )
     (last,) = call(
-        functools.partial(unpack_kernel, plan),
-        [last],
-        [wavefield.shape],
-        flops=5_000_000,
-        name="unpack",
+        functools.partial(unpack_kernel, plan), [last], [wavefield.shape], flops=5_000_000
     )
     scale = 1.0 / math.sqrt(freq_total)
     image = jnp.concatenate([sum_over(image_head, "freq"), sum_over(image_tail, "freq")]) * scale
@@ -612,7 +603,7 @@
 def solution(mesh):
     placed = (P("freq", None, "gx", "gy"), P(None, ("gx", "freq"), "gy"))
     return jax.shard_map(
-        per_device,
+        migrated,
         mesh=mesh,
         in_specs=placed,
         out_specs=(P(None, "gx", "gy"), P("freq", None, "gx", "gy")),

time: 53.8 us -> 53.8 us (level)
  no operation moved by 1% of the time
where the time goes in v5:
time: 53.8 us; the launch traced here: 53.6 us
  Pallas kernels  30.5 us (57%)
  starting transfers between devices  9.97 us (19%)
  waiting for transfers between devices  9.7 us (18%)
  local copies, waits for them, and re-layouts  1.94 us (4%)
  other arithmetic  0.76 us (1%)
  between operations  0.72 us (1%)
    pallas_call x7, Pallas kernels, call(): pl.pallas_call(kernel, out_shape=[jax.ShapeDtypeStruct(s, jnp.float32) fo...  30.5 us
    ppermute x4, waiting for transfers between devices, swap(): return lax.ppermute(value, axis, pairs)  7.09 us
    ppermute x4, starting transfers between devices, swap(): return lax.ppermute(value, axis, pairs)  6.31 us
    ppermute x2, starting transfers between devices, sum_over(): lax.ppermute(value, axis, [(i, i ^ width) for i in range(count)])  2.11 us
    unnamed x4, local copies, waits for them, and re-layouts  1.94 us
    ppermute x1, waiting for transfers between devices, gathered(): lax.ppermute(sent, axis, [(i, i ^ width) for i in range(count)])  1.73 us
    ppermute x1, starting transfers between devices, gathered(): lax.ppermute(sent, axis, [(i, i ^ width) for i in range(count)])  1.56 us
  transfers between devices with their start and end apart: 7, of which 5 were waited for; matrix products, arithmetic and copies ran while one was open for 0% of the time, Pallas kernels for 23%

profile of v5, /device:TPU:20, one launch (start us, length us, event | category | flops | bytes accessed | tf_op | source)
XLA Modules:
  0.0 53.6 jit_solution(10749638964019257703)
XLA Ops:
  0.6 1.6 %collective-permute-start = (f32[4,64,128]{2,1,0:T(8,128)}, f32[4,64,128]{2,1,0:T(8,128)S(1)}, u32[]{:S(2)}, u32[]{:S(2)}) collective-permute-start(f32[4,64,128]{2,1,0:T(8,128)} %speed.1), channel_id=1, source_target_pairs={{0,16},{16,0},{1,17},{17,1},{2,18},{18,2},{3,19},{19,3},{4,20},{20... | collective-permute-start | bytes 393224 | tf_op jit(solution)/shard_map/ppermute | solution.py:503
  2.2 0.0 copy-start
  2.2 1.0 %copy-done = f32[4,2,128,128]{3,2,1,0:T(8,128)S(1)} copy-done((f32[4,2,128,128]{3,2,1,0:T(8,128)S(1)}, f32[4,2,128,128]{3,2,1,0:T(8,128)}, u32[]{:S(2)}) %copy-start) | copy-done | bytes 524312
  3.2 0.0 copy-start.1
  3.2 0.9 %copy-done.1 = f32[4,64,128]{2,1,0:T(8,128)S(1)} copy-done((f32[4,64,128]{2,1,0:T(8,128)S(1)}, f32[4,64,128]{2,1,0:T(8,128)}, u32[]{:S(2)}) %copy-start.1) | copy-done | bytes 131096
  4.1 0.3 shard_map.41
  4.4 1.7 %collective-permute-done.refs_3_ = f32[4,64,128]{2,1,0:T(8,128)S(1)} collective-permute-done((f32[4,64,128]{2,1,0:T(8,128)}, f32[4,64,128]{2,1,0:T(8,128)S(1)}, u32[]{:S(2)}, u32[]{:S(2)}) %collective-permute-start) | collective-permute-done | bytes 131104 | tf_op jit(solution)/shard_map/ppermute | solution.py:503
  6.1 0.2 shard_map.42
  6.3 1.6 %collective-permute-start.1 = (f32[3,128,128]{2,1,0:T(8,128)S(1)}, f32[3,128,128]{2,1,0:T(8,128)S(1)}, u32[]{:S(2)}, u32[]{:S(2)}) collective-permute-start(f32[3,128,128]{2,1,0:T(8,128)S(1)} %get-tuple-element.25), channel_id=1, source_target_pairs={{0,1},{1,0},{2,3},{3,2},{4,5},{5,4},{6,7},{7,6},{8,9},{9,8},{10,11... | collective-permute-start | bytes 589832 | tf_op jit(solution)/shard_map/ppermute | solution.py:494
  8.0 1.9 %collective-permute-start.2 = (f32[3,128,128]{2,1,0:T(8,128)S(1)}, f32[3,128,128]{2,1,0:T(8,128)S(1)}, u32[]{:S(2)}, u32[]{:S(2)}) collective-permute-start(f32[3,128,128]{2,1,0:T(8,128)S(1)} %get-tuple-element.26), channel_id=1, source_target_pairs={{1,2},{2,1},{5,6},{6,5},{9,10},{10,9},{13,14},{14,13},{17,18},{18,... | collective-permute-start | bytes 589832 | tf_op jit(solution)/shard_map/ppermute | solution.py:494
  9.9 2.3 %collective-permute-done.1.got_a = f32[3,128,128]{2,1,0:T(8,128)S(1)} collective-permute-done((f32[3,128,128]{2,1,0:T(8,128)S(1)}, f32[3,128,128]{2,1,0:T(8,128)S(1)}, u32[]{:S(2)}, u32[]{:S(2)}) %collective-permute-start.1) | collective-permute-done | bytes 196640 | tf_op jit(solution)/shard_map/ppermute | solution.py:494
  12.2 3.3 %collective-permute-done.2.got_b = f32[3,128,128]{2,1,0:T(8,128)S(1)} collective-permute-done((f32[3,128,128]{2,1,0:T(8,128)S(1)}, f32[3,128,128]{2,1,0:T(8,128)S(1)}, u32[]{:S(2)}, u32[]{:S(2)}) %collective-permute-start.2) | collective-permute-done | bytes 196640 | tf_op jit(solution)/shard_map/ppermute | solution.py:494
  15.5 2.3 %shard_map.43 = (f32[3,6,128,128]{3,2,1,0:T(8,128)S(1)}, f32[3,6,32,128]{3,2,1,0:T(8,128)S(1)}, f32[3,6,32,128]{3,2,1,0:T(8,128)S(1)}) custom-call(f32[4,2,128,128]{3,2,1,0:T(8,128)S(1)} %get-tuple-element.20.src, f32[4,128,128]{2,1,0:T(8,128)S(1)} %get-tuple-element.24.slow, f32[3,128,128]{2,1,0:T(8,128)S(1)} %collective-permute-done.1.got_a, ...), custom_call_target="tpu_custom_call" | custom-call | bytes 2949120 | tf_op jit(solution)/shard_map/pallas_call | solution.py:523
  17.8 0.1 collective-permute-start.3
  17.9 2.7 %collective-permute-start.4 = (f32[3,6,32,128]{3,2,1,0:T(8,128)S(1)}, f32[3,6,32,128]{3,2,1,0:T(8,128)S(1)}, u32[]{:S(2)}, u32[]{:S(2)}) collective-permute-start(f32[3,6,32,128]{3,2,1,0:T(8,128)S(1)} %get-tuple-element.29), channel_id=1, source_target_pairs={{4,8},{8,4},{5,9},{9,5},{6,10},{10,6},{7,11},{11,7},{20,24},{24,20... | collective-permute-start | bytes 884744 | tf_op jit(solution)/shard_map/ppermute | solution.py:494
  20.6 3.9 %shard_map.44 = (f32[2,6,112,128]{3,2,1,0:T(8,128)S(1)}, f32[8,2,2,6,8,128]{5,4,3,2,1,0:T(8,128)S(1)}, f32[112,128]{1,0:T(8,128)S(1)}) custom-call(f32[3,6,128,128]{3,2,1,0:T(8,128)S(1)} %get-tuple-element.27.tile.refs_0_), custom_call_target="tpu_custom_call" | custom-call | flops 10000000 | bytes 2711552 | tf_op jit(solution)/shard_map/pallas_call | solution.py:523
  24.5 0.0 collective-permute-done.3.refs_1_
  24.5 1.5 %collective-permute-done.4.refs_2_ = f32[3,6,32,128]{3,2,1,0:T(8,128)S(1)} collective-permute-done((f32[3,6,32,128]{3,2,1,0:T(8,128)S(1)}, f32[3,6,32,128]{3,2,1,0:T(8,128)S(1)}, u32[]{:S(2)}, u32[]{:S(2)}) %collective-permute-start.4) | collective-permute-done | bytes 294944 | tf_op jit(solution)/shard_map/ppermute | solution.py:494
  26.0 15.7 %shard_map.45 = (f32[3,128,128]{2,1,0:T(8,128)S(1)}, f32[2,6,144,128]{3,2,1,0:T(8,128)S(1)}, f32[6,128,128]{2,1,0:T(8,128)S(1)}) custom-call(f32[3,6,128,128]{3,2,1,0:T(8,128)S(1)} %get-tuple-element.27.tile.refs_0_, f32[3,6,32,128]{3,2,1,0:T(8,128)S(1)} %collective-permute-done.3.refs_1_, f32[3,6,32,128]{3,2,1,0:T(8,128)S(1)} %collective-permute-done.4.refs_2_, ...), custom_call_target="tpu_custom_call" | custom-call | flops 30000000 | bytes 4775936 | tf_op jit(solution)/shard_map/pallas_call | solution.py:523
  41.7 1.5 %collective-permute-start.5 = (f32[3,128,128]{2,1,0:T(8,128)S(1)}, f32[3,128,128]{2,1,0:T(8,128)S(1)}, u32[]{:S(2)}, u32[]{:S(2)}) collective-permute-start(f32[3,128,128]{2,1,0:T(8,128)S(1)} %get-tuple-element.33), channel_id=1, source_target_pairs={{0,16},{16,0},{1,17},{17,1},{2,18},{18,2},{3,19},{19,3},{4,20},{20... | collective-permute-start | bytes 589832 | tf_op jit(solution)/shard_map/ppermute | solution.py:512
  43.2 5.2 %shard_map.46 = (f32[1,128,128]{2,1,0:T(8,128)S(1)}, f32[2,6,128,128]{3,2,1,0:T(8,128)S(1)}) custom-call(f32[2,6,144,128]{3,2,1,0:T(8,128)S(1)} %get-tuple-element.34.refs_0_, f32[6,128,128]{2,1,0:T(8,128)S(1)} %get-tuple-element.35.refs_1_), custom_call_target="tpu_custom_call" | custom-call | flops 30000000 | bytes 2129920 | tf_op jit(solution)/shard_map/pallas_call | solution.py:523
  48.5 0.6 %collective-permute-start.6 = (f32[1,128,128]{2,1,0:T(8,128)S(1)}, f32[1,128,128]{2,1,0:T(8,128)S(1)}, u32[]{:S(2)}, u32[]{:S(2)}) collective-permute-start(f32[1,128,128]{2,1,0:T(8,128)S(1)} %get-tuple-element.36), channel_id=1, source_target_pairs={{0,16},{16,0},{1,17},{17,1},{2,18},{18,2},{3,19},{19,3},{4,20},{20... | collective-permute-start | bytes 196616 | tf_op jit(solution)/shard_map/ppermute | solution.py:512
  49.1 2.9 %shard_map.47 = f32[4,2,128,128]{3,2,1,0:T(8,128)} custom-call(f32[2,6,128,128]{3,2,1,0:T(8,128)S(1)} %get-tuple-element.37.fresh), custom_call_target="tpu_custom_call" | custom-call | flops 5000000 | bytes 1310720 | tf_op jit(solution)/shard_map/pallas_call | solution.py:523
  51.9 0.9 %collective-permute-done.6 = f32[1,128,128]{2,1,0:T(8,128)S(1)} collective-permute-done((f32[1,128,128]{2,1,0:T(8,128)S(1)}, f32[1,128,128]{2,1,0:T(8,128)S(1)}, u32[]{:S(2)}, u32[]{:S(2)}) %collective-permute-start.6) | collective-permute-done | bytes 65568 | tf_op jit(solution)/shard_map/ppermute | solution.py:512
  52.8 0.0 collective-permute-done.5
  52.8 0.7 %maximum_multiply_fusion = f32[4,128,128]{2,1,0:T(8,128)} fusion(f32[1,128,128]{2,1,0:T(8,128)S(1)} %add.7, f32[3,128,128]{2,1,0:T(8,128)S(1)} %add.6), kind=kLoop, calls=%fused_computation | loop fusion | flops 131072 | bytes 524288 | tf_op jit(solution)/shard_map/mul | solution.py:599
  (2 shorter events, 0.0 us)
Async XLA Ops:
  0.6 5.5 %collective-permute-start = (f32[4,64,128]{2,1,0:T(8,128)}, f32[4,64,128]{2,1,0:T(8,128)S(1)}, u32[]{:S(2)}, u32[]{:S(2)}) collective-permute-start(f32[4,64,128]{2,1,0:T(8,128)} %speed.1), channel_id=1, source_target_pairs={{0,16},{16,0},{1,17},{17,1},{2,18},{18,2},{3,19},{19,3},{4,20},{20... | collective-permute-start | bytes 393224 | tf_op jit(solution)/shard_map/ppermute | solution.py:503
  2.2 1.0 %copy-start = (f32[4,2,128,128]{3,2,1,0:T(8,128)S(1)}, f32[4,2,128,128]{3,2,1,0:T(8,128)}, u32[]{:S(2)}) copy-start(f32[4,2,128,128]{3,2,1,0:T(8,128)} %src.1) | copy-start | bytes 1572868
  3.2 0.9 %copy-start.1 = (f32[4,64,128]{2,1,0:T(8,128)S(1)}, f32[4,64,128]{2,1,0:T(8,128)}, u32[]{:S(2)}) copy-start(f32[4,64,128]{2,1,0:T(8,128)} %speed.1) | copy-start | bytes 393220
  6.3 5.9 %collective-permute-start.1 = (f32[3,128,128]{2,1,0:T(8,128)S(1)}, f32[3,128,128]{2,1,0:T(8,128)S(1)}, u32[]{:S(2)}, u32[]{:S(2)}) collective-permute-start(f32[3,128,128]{2,1,0:T(8,128)S(1)} %get-tuple-element.25), channel_id=1, source_target_pairs={{0,1},{1,0},{2,3},{3,2},{4,5},{5,4},{6,7},{7,6},{8,9},{9,8},{10,11... | collective-permute-start | bytes 589832 | tf_op jit(solution)/shard_map/ppermute | solution.py:494
  8.0 7.6 %collective-permute-start.2 = (f32[3,128,128]{2,1,0:T(8,128)S(1)}, f32[3,128,128]{2,1,0:T(8,128)S(1)}, u32[]{:S(2)}, u32[]{:S(2)}) collective-permute-start(f32[3,128,128]{2,1,0:T(8,128)S(1)} %get-tuple-element.26), channel_id=1, source_target_pairs={{1,2},{2,1},{5,6},{6,5},{9,10},{10,9},{13,14},{14,13},{17,18},{18,... | collective-permute-start | bytes 589832 | tf_op jit(solution)/shard_map/ppermute | solution.py:494
  17.8 6.7 %collective-permute-start.3 = (f32[3,6,32,128]{3,2,1,0:T(8,128)S(1)}, f32[3,6,32,128]{3,2,1,0:T(8,128)S(1)}, u32[]{:S(2)}, u32[]{:S(2)}) collective-permute-start(f32[3,6,32,128]{3,2,1,0:T(8,128)S(1)} %get-tuple-element.28), channel_id=1, source_target_pairs={{0,4},{4,0},{8,12},{12,8},{1,5},{5,1},{9,13},{13,9},{2,6},{6,2},{1... | collective-permute-start | bytes 884744 | tf_op jit(solution)/shard_map/ppermute | solution.py:494
  17.9 8.0 %collective-permute-start.4 = (f32[3,6,32,128]{3,2,1,0:T(8,128)S(1)}, f32[3,6,32,128]{3,2,1,0:T(8,128)S(1)}, u32[]{:S(2)}, u32[]{:S(2)}) collective-permute-start(f32[3,6,32,128]{3,2,1,0:T(8,128)S(1)} %get-tuple-element.29), channel_id=1, source_target_pairs={{4,8},{8,4},{5,9},{9,5},{6,10},{10,6},{7,11},{11,7},{20,24},{24,20... | collective-permute-start | bytes 884744 | tf_op jit(solution)/shard_map/ppermute | solution.py:494
  41.7 11.1 %collective-permute-start.5 = (f32[3,128,128]{2,1,0:T(8,128)S(1)}, f32[3,128,128]{2,1,0:T(8,128)S(1)}, u32[]{:S(2)}, u32[]{:S(2)}) collective-permute-start(f32[3,128,128]{2,1,0:T(8,128)S(1)} %get-tuple-element.33), channel_id=1, source_target_pairs={{0,16},{16,0},{1,17},{17,1},{2,18},{18,2},{3,19},{19,3},{4,20},{20... | collective-permute-start | bytes 589832 | tf_op jit(solution)/shard_map/ppermute | solution.py:512
  48.5 4.3 %collective-permute-start.6 = (f32[1,128,128]{2,1,0:T(8,128)S(1)}, f32[1,128,128]{2,1,0:T(8,128)S(1)}, u32[]{:S(2)}, u32[]{:S(2)}) collective-permute-start(f32[1,128,128]{2,1,0:T(8,128)S(1)} %get-tuple-element.36), channel_id=1, source_target_pairs={{0,16},{16,0},{1,17},{17,1},{2,18},{18,2},{3,19},{19,3},{4,20},{20... | collective-permute-start | bytes 196616 | tf_op jit(solution)/shard_map/ppermute | solution.py:512
